TPU v7x, 32 devices: a whole 2x2x4 slice. The times are simulated.
32 devices in a mesh: ctx: 8 (over z, x), tp: 4 (over y, core).
Axes of the slice: x: 2, y: 2, z: 4, core: 2. Of those that a mesh axis runs over, the one named last changes fastest.
Arguments:
- residual: bfloat16 [1024, 4096], P('ctx', 'tp')
- mixer_input: bfloat16 [1024, 4096], P('ctx', 'tp')
- gate_input: bfloat16 [1024, 4096], P('ctx', 'tp'), may hold values from -6 to 6
- state_proj: bfloat16 [1024, 32], P('ctx'), may hold values from -6 to 6
- step_raw: float32 [1024, 64], P('ctx', 'tp'), may hold values from -5 to 5
- conv_weight: float32 [4, 4096], P(None, 'tp'), may hold values from -3 to 3
- conv_state_weight: float32 [4, 32], replicated, may hold values from -3 to 3
- step_bias: float32 [64], P('tp'), may hold values from -3.5 to 0.5
- decay_log: float32 [64], P('tp')
- skip_gain: float32 [64], P('tp'), may hold values from 0.5 to 1.5
- mixer_gain: float32 [4096], P('tp'), may hold values from 0.5 to 1.5
- out_weight: bfloat16 [4096, 4096], P('tp', 'ctx'), may hold values from -0.09375 to 0.09375
- feed_gain: float32 [4096], P('tp'), may hold values from 0.5 to 1.5
- expert_gate: bfloat16 [8, 4096, 7168], P('ctx', 'tp'), may hold values from -0.09375 to 0.09375
- expert_up: bfloat16 [8, 4096, 7168], P('ctx', 'tp'), may hold values from -0.09375 to 0.09375
- expert_down: bfloat16 [8, 7168, 4096], P('ctx', None, 'tp'), may hold values from -0.0625 to 0.0625
- expert_ids: int32 [1024, 2], P('ctx'), may hold values from 0 to 7, all different within a row; in each aligned block of 128 rows (0 to 127, 128 to 255, ...) at most 36 rows name the same one
- expert_weights: float32 [1024, 2], P('ctx'), may hold values from 0.1 to 0.9
Outputs:
- block_out: bfloat16 [1024, 4096], P('ctx', 'tp')
Inputs may be any that keep to these rules, and one draw needn't show every extreme that they name: `expert_ids`: in each aligned block of 128 rows no expert is named more than 36 times, and some block reaches 36; the two experts of a row differ.
All inputs are finite; a program needn't handle non-finite values.
Results may differ from a plain program's by a relative error of at most 0.014.
Values may be sent and summed in bfloat16 or wider, within the bound.
A program may use at most 128 MiB of HBM per device.

v0:
```python
import functools

import jax
import jax.numpy as jnp
from jax import lax
from jax.experimental import pallas as pl
from jax.experimental.pallas import tpu as pltpu
from jax.sharding import PartitionSpec as P


EXPERTS = 8
CAP = 36


EPSILON = 1e-05


def passed_along(value, axis, steps):
    count = lax.axis_size(axis)
    first, last = (max(0, -steps), min(count, count - steps))
    return lax.ppermute(value, axis, [(source, source + steps) for source in range(first, last)])


def swapped(value, distance):
    return lax.ppermute(value, "tp", [(p, p ^ distance) for p in range(lax.axis_size("tp"))])


def rotated(value, steps):
    count = lax.axis_size("ctx")
    return lax.ppermute(value, "ctx", [(c, (c + steps) % count) for c in range(count)])


def tensor_total(value):
    return (value + swapped(value, 1)) + (swapped(value, 2) + swapped(value, 3))


def entering(decay, fresh, axis):
    peers, position = (lax.axis_size(axis), lax.axis_index(axis))
    packed = jnp.concatenate([fresh, decay[None, :]], axis=0).astype(jnp.bfloat16)
    if peers == EXPERTS:
        total, carry = (jnp.zeros_like(fresh), jnp.ones_like(decay)[None, :])
        for distance in range(1, peers):
            part = passed_along(packed, axis, distance).astype(jnp.float32)
            total = total + carry * part[:-1]
            carry = carry * part[-1:]
        return total
    everything = lax.all_gather(packed, axis).astype(jnp.float32)

    def step(k, before):
        part = everything[k]
        return jnp.where(k < position, part[-1:] * before + part[:-1], before)

    return lax.fori_loop(0, peers, step, jnp.zeros_like(fresh))


def causal_filter(previous, current, kernel):
    joined = jnp.concatenate([previous, current], axis=0)
    length = current.shape[0]
    total = jnp.zeros(current.shape, jnp.float32)
    for offset in range(kernel.shape[0]):
        total = total + kernel[offset][None, :] * joined[offset : offset + length]
    return jax.nn.silu(total)


def local_terms(values, writer, reader, step_size, log_decay):
    length = values.shape[0]
    cumulative = jnp.cumsum(log_decay, axis=0)
    scores = jnp.dot(reader, writer.T, precision=lax.Precision.HIGHEST)
    order = jnp.arange(length)
    causal = (order[:, None] >= order[None, :])[:, :, None]
    spans = cumulative[:, None, :] - cumulative[None, :, :]
    factor = jnp.where(causal, jnp.exp(jnp.where(causal, spans, 0.0)), 0.0)
    factor = factor * step_size[None, :, :] * scores[:, :, None]
    inside = jnp.einsum("tsh,shp->thp", factor, values, precision=lax.Precision.HIGHEST)
    tail = cumulative[length - 1]
    ending = jnp.exp(tail[None, :] - cumulative) * step_size
    weighted = (ending[:, :, None] * values).reshape(length, -1)
    fresh = jnp.dot(writer.T, weighted, precision=lax.Precision.HIGHEST)
    return (inside, cumulative, fresh, tail)


SUB = 16
CHUNK = 256
MESH = pl.DeviceIdType.MESH


def remote(source, target, send, receive, device):
    return pltpu.make_async_remote_copy(
        src_ref=source,
        dst_ref=target,
        send_sem=send,
        recv_sem=receive,
        device_id=device,
        device_id_type=MESH,
    )


def unfold(count, extra, fold, part):
    j = lax.broadcasted_iota(jnp.int32, (count * extra, count * SUB), 0)
    i = lax.broadcasted_iota(jnp.int32, (count * extra, count * SUB), 1)
    return (i == j * fold + part).astype(jnp.bfloat16)


def refold(count, extra, fold, part):
    j = lax.broadcasted_iota(jnp.int32, (count * SUB, count * extra), 1)
    i = lax.broadcasted_iota(jnp.int32, (count * SUB, count * extra), 0)
    return (i == j * fold + part).astype(jnp.bfloat16)


def expert_kernel(
    peers,
    expert_input,
    picker,
    hidden,
    weights_high,
    weights_low,
    gate,
    up,
    down,
    out,
    gate_tiles,
    up_tiles,
    down_tiles,
    packed,
    packed_extra,
    rows,
    rows_extra,
    answers,
    answers_extra,
    first,
    first_in,
    far,
    far_in,
    near_in,
    active,
    active_beside,
    active_across,
    active_diagonal,
    total,
    tile_sem,
    home_send,
    home_receive,
    pair_send,
    pair_receive,
):
    ctx, tp = lax.axis_index("ctx"), lax.axis_index("tp")
    beside = tp + 1 - 2 * (tp % 2)
    across = (tp + 2) % 4
    diagonal = 3 - tp
    width = rows.shape[1]
    chunks = first.shape[1]
    hidden_width = chunks * CHUNK
    main = packed.shape[0] // peers
    extra = (rows.shape[0] - peers * main) // peers
    fold = SUB // extra
    piece = width // fold

    places = ((diagonal, across, beside, tp), (diagonal, across, beside, tp), (tp, beside, across, diagonal))

    def tile(kind, place, j):
        span = pl.ds(pl.multiple_of(places[kind][place] * hidden_width + j * CHUNK, CHUNK), CHUNK)
        source = (gate, up, down)[kind]
        source = source.at[0, span, :] if kind == 2 else source.at[0, :, span]
        target = (gate_tiles, up_tiles, down_tiles)[kind].at[place, j]
        return pltpu.make_async_copy(source, target, tile_sem.at[4 * kind + place, j])

    def start_group(chosen):
        def body(j, carry):
            for kind, place in chosen:
                tile(kind, place, j).start()
            return carry

        lax.fori_loop(0, chunks, body, 0)

    start_group([(kind, place) for place in (0, 1) for kind in (0, 1)])
    start_group([(kind, place) for place in (2, 3) for kind in (0, 1)])
    start_group([(2, place) for place in range(4)])

    barrier = pltpu.get_barrier_semaphore()
    for distance in range(1, peers):
        pl.semaphore_signal(
            barrier, inc=1, device_id={"ctx": (ctx + distance) % peers}, device_id_type=MESH
        )
    for other in (beside, across, diagonal):
        pl.semaphore_signal(barrier, inc=1, device_id={"tp": other}, device_id_type=MESH)

    picked = jnp.dot(picker[...], expert_input[...], preferred_element_type=jnp.float32)
    packed[...] = picked[: peers * main].astype(jnp.bfloat16)
    tail = picked[peers * main :].astype(jnp.bfloat16)
    folded = jnp.zeros((peers * SUB, piece), jnp.float32)
    for part in range(fold):
        folded = folded + jnp.dot(
            refold(peers, extra, fold, part),
            tail[:, part * piece : (part + 1) * piece],
            preferred_element_type=jnp.float32,
        )
    packed_extra[...] = folded.astype(jnp.bfloat16)
    pl.semaphore_wait(barrier, peers - 1 + 3)

    def travel(sources, targets, sign, base):
        copies = []
        for kind, (source, target) in enumerate(zip(sources, targets)):
            size = (main, SUB)[kind]
            for distance in range(1, peers):
                block = pl.ds(distance * size, size)
                copies.append(
                    remote(
                        source.at[block],
                        target.at[block],
                        home_send.at[base + kind, distance],
                        home_receive.at[base + kind, distance],
                        {"ctx": (ctx + sign * distance + peers) % peers},
                    )
                )
        return copies

    outward = travel((packed, packed_extra), (rows, rows_extra), 1, 0)
    for copy in outward:
        copy.start()
    rows[:main] = packed[:main]
    rows_extra[:SUB] = packed_extra[:SUB]
    for copy in outward:
        copy.wait_recv()
    landed = rows_extra[...]
    for part in range(fold):
        rows[peers * main :, part * piece : (part + 1) * piece] = jnp.dot(
            unfold(peers, extra, fold, part), landed, preferred_element_type=jnp.float32
        ).astype(jnp.bfloat16)

    def pair(kind, j, source, target, other):
        return remote(source, target, pair_send.at[kind, j], pair_receive.at[kind, j], {"tp": other})

    both = (gate_tiles, up_tiles)

    def product(which, place, j):
        tile(which, place, j).wait()
        return jnp.dot(rows[...], both[which][place, j], preferred_element_type=jnp.float32)

    def first_copy(which, j):
        return pair(which, j, first.at[which, j], first_in.at[which, j], beside)

    def far_copy(which, j):
        return pair(2 + which, j, far.at[which, j], far_in.at[which, j], across)

    def near_copy(which, j):
        return pair(4 + which, j, first.at[which, j], near_in.at[which, j], beside)

    def beside_copy(j):
        return pair(6, j, active.at[j], active_beside.at[j], beside)

    def across_copy(j):
        return pair(7, j, active.at[j], active_across.at[j], across)

    def diagonal_copy(j):
        return pair(8, j, active_across.at[j], active_diagonal.at[j], beside)

    def far_step(j, carry):
        for which in range(2):
            first[which, j] = product(which, 0, j).astype(jnp.bfloat16)
            first_copy(which, j).start()
        for which in range(2):
            mine = product(which, 1, j)
            first_copy(which, j).wait_recv()
            far[which, j] = (mine + first_in[which, j].astype(jnp.float32)).astype(jnp.bfloat16)
            far_copy(which, j).start()
        return carry

    lax.fori_loop(0, chunks, far_step, 0)

    def near_step(j, carry):
        for which in range(2):
            mine = product(which, 2, j).astype(jnp.bfloat16)
            first_copy(which, j).wait_send()
            first[which, j] = mine
            near_copy(which, j).start()
        return carry

    lax.fori_loop(0, chunks, near_step, 0)
    total[...] = jnp.zeros_like(total)

    def lowered(source, place, j):
        tile(2, place, j).wait()
        total[...] += jnp.dot(source[j], down_tiles[place, j], preferred_element_type=jnp.float32)

    def own_step(j, carry):
        sums = []
        for which in range(2):
            mine = product(which, 3, j).astype(jnp.bfloat16).astype(jnp.float32)
            near_copy(which, j).wait_recv()
            mine = mine + near_in[which, j].astype(jnp.float32)
            far_copy(which, j).wait_recv()
            sums.append(mine + far_in[which, j].astype(jnp.float32))
        active[j] = (jax.nn.silu(sums[0]) * sums[1]).astype(jnp.bfloat16)
        across_copy(j).start()
        beside_copy(j).start()
        lowered(active, 0, j)
        beside_copy(j).wait_recv()
        lowered(active_beside, 1, j)
        return carry

    lax.fori_loop(0, chunks, own_step, 0)

    def last_step(j, carry):
        across_copy(j).wait_recv()
        diagonal_copy(j).start()
        lowered(active_across, 2, j)
        diagonal_copy(j).wait_recv()
        lowered(active_diagonal, 3, j)
        return carry

    lax.fori_loop(0, chunks, last_step, 0)

    for copy in outward:
        copy.wait_send()
    packed[...] = total[: peers * main].astype(jnp.bfloat16)
    tail = total[peers * main :].astype(jnp.bfloat16)
    folded = jnp.zeros((peers * SUB, piece), jnp.float32)
    for part in range(fold):
        folded = folded + jnp.dot(
            refold(peers, extra, fold, part),
            tail[:, part * piece : (part + 1) * piece],
            preferred_element_type=jnp.float32,
        )
    packed_extra[...] = folded.astype(jnp.bfloat16)
    homeward = travel((packed, packed_extra), (answers, answers_extra), -1, 2)
    for copy in homeward:
        copy.start()
    answers[:main] = packed[:main]
    answers_extra[:SUB] = packed_extra[:SUB]

    def drain(j, carry):
        for which in range(2):
            far_copy(which, j).wait_send()
            near_copy(which, j).wait_send()
        beside_copy(j).wait_send()
        across_copy(j).wait_send()
        diagonal_copy(j).wait_send()
        return carry

    lax.fori_loop(0, chunks, drain, 0)
    for copy in homeward:
        copy.wait_recv()
    landed = answers_extra[...]
    for part in range(fold):
        answers[peers * main :, part * piece : (part + 1) * piece] = jnp.dot(
            unfold(peers, extra, fold, part), landed, preferred_element_type=jnp.float32
        ).astype(jnp.bfloat16)
    routed = jnp.dot(weights_high[...], answers[...], preferred_element_type=jnp.float32)
    routed = routed + jnp.dot(weights_low[...], answers[...], preferred_element_type=jnp.float32)
    out[...] = (hidden[...].astype(jnp.float32) + routed).astype(jnp.bfloat16)
    for copy in homeward:
        copy.wait_send()


def experts_direct(expert_input, hidden, expert_ids, expert_weights, gate, up, down):
    peers = lax.axis_size("ctx")
    ctx = lax.axis_index("ctx")
    tokens, width = expert_input.shape
    hidden_width = gate.shape[2] // 4
    chunks = hidden_width // CHUNK
    main = CAP // SUB * SUB
    extra = CAP - main
    count = peers * CAP
    flat = expert_ids.reshape(-1)
    matches = (flat[:, None] == jnp.arange(EXPERTS)[None, :]).astype(jnp.int32)
    slots = jnp.sum((jnp.cumsum(matches, axis=0) - matches) * matches, axis=1)
    places = (flat - ctx) % EXPERTS
    targets = jnp.where(
        slots < main, places * main + slots, peers * main + places * extra + slots - main
    ).reshape(tokens, -1)
    chosen = targets[:, :, None] == jnp.arange(count)[None, None, :]
    weights = jnp.sum(jnp.where(chosen, expert_weights[:, :, None], 0.0), axis=1)
    weights_high = weights.astype(jnp.bfloat16)
    weights_low = (weights - weights_high.astype(jnp.float32)).astype(jnp.bfloat16)
    picker = jnp.any(
        targets[None, :, :] == jnp.arange(count)[:, None, None], axis=2
    ).astype(jnp.bfloat16)
    vmem = pl.BlockSpec(memory_space=pltpu.VMEM)
    anywhere = pl.BlockSpec(memory_space=pl.ANY)
    block = (chunks, count, CHUNK)
    low = jnp.bfloat16
    return pl.pallas_call(
        functools.partial(expert_kernel, peers),
        out_shape=jax.ShapeDtypeStruct((tokens, width), low),
        in_specs=[vmem] * 5 + [anywhere] * 3,
        out_specs=vmem,
        scratch_shapes=[
            pltpu.VMEM((4, chunks, width, CHUNK), low),
            pltpu.VMEM((4, chunks, width, CHUNK), low),
            pltpu.VMEM((4, chunks, CHUNK, width), low),
            pltpu.VMEM((peers * main, width), low),
            pltpu.VMEM((peers * SUB, width * extra // SUB), low),
            pltpu.VMEM((count, width), low),
            pltpu.VMEM((peers * SUB, width * extra // SUB), low),
            pltpu.VMEM((count, width), low),
            pltpu.VMEM((peers * SUB, width * extra // SUB), low),
            pltpu.VMEM((2,) + block, low),
            pltpu.VMEM((2,) + block, low),
            pltpu.VMEM((2,) + block, low),
            pltpu.VMEM((2,) + block, low),
            pltpu.VMEM((2,) + block, low),
            pltpu.VMEM(block, low),
            pltpu.VMEM(block, low),
            pltpu.VMEM(block, low),
            pltpu.VMEM(block, low),
            pltpu.VMEM((count, width), jnp.float32),
            pltpu.SemaphoreType.DMA((12, chunks)),
            pltpu.SemaphoreType.DMA((4, peers)),
            pltpu.SemaphoreType.DMA((4, peers)),
            pltpu.SemaphoreType.DMA((9, chunks)),
            pltpu.SemaphoreType.DMA((9, chunks)),
        ],
        compiler_params=pltpu.CompilerParams(
            collective_id=0, has_side_effects=True, vmem_limit_bytes=66_000_000
        ),
        name="experts",
    )(expert_input, picker, hidden, weights_high, weights_low, gate, up, down)


def body(
    residual,
    mixer_input,
    gate_input,
    state_proj,
    step_raw,
    conv_weight,
    conv_state_weight,
    step_bias,
    decay_log,
    skip_gain,
    mixer_gain,
    out_weight,
    feed_gain,
    expert_gate,
    expert_up,
    expert_down,
    expert_ids,
    expert_weights,
):
    tensor_count = lax.axis_size("tp")
    context_count = lax.axis_size("ctx")
    tokens = mixer_input.shape[0]
    channels = mixer_input.shape[1]
    states = state_proj.shape[1] // 2
    heads_local = step_raw.shape[1]
    head_size = channels // heads_local
    taps = conv_weight.shape[0]
    joined = jnp.concatenate([mixer_input, state_proj], axis=1)
    previous = passed_along(joined[tokens - (taps - 1) :], "ctx", 1)
    kernel = jnp.concatenate([conv_weight, conv_state_weight], axis=1)
    filtered = causal_filter(previous.astype(jnp.float32), joined.astype(jnp.float32), kernel)
    values = filtered[:, :channels].reshape(tokens, heads_local, head_size)
    writer = filtered[:, channels : channels + states]
    reader = filtered[:, channels + states :]
    step_size = jax.nn.softplus(step_raw + step_bias[None, :])
    log_decay = -step_size * jnp.exp(decay_log)[None, :]
    inside, cumulative, fresh, tail = local_terms(values, writer, reader, step_size, log_decay)

    incoming = entering(jnp.repeat(jnp.exp(tail), head_size), fresh, "ctx")
    carried = (
        jnp.dot(reader, incoming, precision=lax.Precision.HIGHEST).reshape(values.shape)
        * jnp.exp(cumulative)[:, :, None]
    )
    mixed = inside + carried + skip_gain[None, :, None] * values
    gated = mixed.reshape(tokens, channels) * jax.nn.silu(gate_input.astype(jnp.float32))
    tp_index = lax.axis_index("tp")
    core, chip = (tp_index % 2, tp_index // 2)
    scaled = (gated * mixer_gain[None, :]).astype(jnp.bfloat16)
    direct = context_count == EXPERTS
    ctx_index = lax.axis_index("ctx")
    if direct:
        pairs = []
        for plane in range(4):
            block = rotated(scaled, 2 * plane) if plane else scaled
            other = lax.ppermute(block, "ctx", [(c, c ^ 1) for c in range(context_count)])
            pair = jnp.concatenate([block, other], axis=0)
            pairs.append(jnp.dot(pair, out_weight, preferred_element_type=jnp.float32))
        products = jnp.stack(pairs)

        def projected(quarter):
            place = (ctx_index // 2 - quarter) % 4
            return lax.dynamic_index_in_dim(products, place, 0, keepdims=False)

    else:
        everyone = lax.all_gather(scaled, "ctx", axis=0, tiled=True)
        span = everyone.shape[0] // tensor_count

        def projected(quarter):
            rows = lax.dynamic_slice_in_dim(everyone, quarter * span, span, 0)
            return jnp.dot(rows, out_weight, preferred_element_type=jnp.float32)

    square_sum = tensor_total(jnp.sum(gated * gated, axis=1))
    scale = lax.rsqrt(square_sum / (channels * tensor_count) + EPSILON)
    own, beside = (chip * 2 + core, chip * 2 + 1 - core)
    across, diagonal = ((1 - chip) * 2 + core, (1 - chip) * 2 + 1 - core)
    far = swapped(projected(diagonal).astype(jnp.bfloat16), 1)
    far = swapped((projected(across) + far.astype(jnp.float32)).astype(jnp.bfloat16), 2)
    near = swapped(projected(beside).astype(jnp.bfloat16), 1)
    reduced = projected(own) + near.astype(jnp.float32) + far.astype(jnp.float32)
    blocks = context_count // tensor_count
    reduced = reduced.astype(jnp.bfloat16).reshape(blocks, tokens, -1)
    pieces = []
    for j in range(blocks):
        moves = [
            (c * tensor_count + p, (p * blocks + (c + j) % blocks) * tensor_count + c // blocks)
            for c in range(context_count)
            for p in range(tensor_count)
        ]
        if direct:
            block = reduced[j]
        else:
            block = lax.dynamic_index_in_dim(reduced, (ctx_index + j) % blocks, 0, keepdims=False)
        pieces.append(lax.ppermute(block, ("ctx", "tp"), moves))
    stacked = jnp.stack(pieces)
    order = (ctx_index - jnp.arange(blocks)) % blocks
    if blocks == 2:
        first = ctx_index % 2 == 0
        mixer_out = jnp.concatenate(
            [jnp.where(first, pieces[0], pieces[1]), jnp.where(first, pieces[1], pieces[0])], axis=1
        )
    else:
        mixer_out = jnp.take(stacked, order, axis=0).transpose(1, 0, 2).reshape(tokens, -1)
    mixer_out = mixer_out.astype(jnp.float32) * scale[:, None]
    hidden_state = (residual.astype(jnp.float32) + mixer_out).astype(jnp.bfloat16)
    state_float = lax.optimization_barrier(hidden_state).astype(jnp.float32)
    width_total = hidden_state.shape[1] * tensor_count
    feed_sum = tensor_total(jnp.sum(state_float * state_float, axis=1))
    feed_scale = lax.rsqrt(feed_sum / width_total + EPSILON)
    expert_input = (state_float * feed_scale[:, None] * feed_gain[None, :]).astype(jnp.bfloat16)
    if direct:
        return experts_direct(
            expert_input, hidden_state, expert_ids, expert_weights, expert_gate, expert_up, expert_down
        )
    group = context_count // EXPERTS
    width_local = expert_input.shape[1]
    flat_experts = expert_ids.reshape(-1)
    matches = (flat_experts[:, None] == jnp.arange(EXPERTS)[None, :]).astype(jnp.int32)
    slots = jnp.sum((jnp.cumsum(matches, axis=0) - matches) * matches, axis=1)
    places = (flat_experts - ctx_index) % EXPERTS if direct else flat_experts
    targets = (places * CAP + slots).reshape(tokens, -1)
    picker = jnp.any(targets[None, :, :] == jnp.arange(EXPERTS * CAP)[:, None, None], axis=2)
    buffer = jnp.dot(
        picker.astype(jnp.bfloat16), expert_input, preferred_element_type=jnp.float32
    ).astype(jnp.bfloat16)
    outgoing = jnp.broadcast_to(
        buffer.reshape(EXPERTS, 1, CAP, width_local), (EXPERTS, group, CAP, width_local)
    )
    outgoing = outgoing.reshape(EXPERTS * group, CAP, width_local)
    gate_local = expert_gate[0]
    up_local = expert_up[0]
    down_local = expert_down[0]
    sources, items, depth = outgoing.shape
    if direct:
        flattened = jnp.concatenate(
            [outgoing[r] if r == 0 else rotated(outgoing[r], r) for r in range(sources)], axis=0
        )
    else:
        arrived = lax.all_to_all(outgoing, "ctx", split_axis=0, concat_axis=0, tiled=True)
        flattened = arrived.reshape(sources * items, depth)
    hidden = gate_local.shape[1] // tensor_count

    def product(source, weight, quarter):
        columns = lax.dynamic_slice_in_dim(weight, quarter * hidden, hidden, 1)
        return jnp.dot(source, columns, preferred_element_type=jnp.float32)

    fars, nears, rows = ([], [], flattened)
    for weight in (gate_local, up_local):
        far = product(rows, weight, diagonal).astype(jnp.bfloat16)
        far = swapped(far, 1)
        nears.append(swapped(product(rows, weight, beside).astype(jnp.bfloat16), 1))
        far = (product(rows, weight, across) + far.astype(jnp.float32)).astype(jnp.bfloat16)
        far, rows = lax.optimization_barrier((far, rows))
        fars.append(swapped(far, 2))
    gate_share, up_share = (
        product(rows, weight, own).astype(jnp.bfloat16).astype(jnp.float32)
        + near.astype(jnp.float32)
        + far.astype(jnp.float32)
        for weight, near, far in zip((gate_local, up_local), nears, fars)
    )
    share = (jax.nn.silu(gate_share) * up_share).astype(jnp.bfloat16)
    share_across = swapped(share, 2)
    share_beside = swapped(share, 1)

    def lowered(part, quarter):
        rows = lax.dynamic_slice_in_dim(down_local, quarter * hidden, hidden, 0)
        return jnp.dot(part, rows, preferred_element_type=jnp.float32)

    local = lowered(share, own) + lowered(share_beside, beside)
    local, share_across = lax.optimization_barrier((local, share_across))
    share_diagonal = swapped(share_across, 1)
    answer = (
        local
        + lowered(share_across, across)
        + lowered(share_diagonal, diagonal)
    ).astype(jnp.bfloat16)
    answer = answer.reshape(sources, items, depth)
    if direct:
        answers = jnp.stack(
            [answer[r] if r == 0 else rotated(answer[r], -r) for r in range(sources)]
        )
    else:
        answers = lax.all_to_all(answer, "ctx", split_axis=0, concat_axis=0, tiled=True)
    summed = jnp.sum(answers.reshape(EXPERTS, group, CAP, width_local), axis=1, dtype=jnp.float32)
    summed = summed.reshape(EXPERTS * CAP, width_local)
    chosen = jnp.take(summed, targets, axis=0)
    routed = jnp.sum(expert_weights[:, :, None] * chosen, axis=1)
    return (state_float + routed).astype(jnp.bfloat16)


def solution(mesh):
    placed = (
        P("ctx", "tp"),
        P("ctx", "tp"),
        P("ctx", "tp"),
        P("ctx", None),
        P("ctx", "tp"),
        P(None, "tp"),
        P(),
        P("tp"),
        P("tp"),
        P("tp"),
        P("tp"),
        P("tp", "ctx"),
        P("tp"),
        P("ctx", "tp", None),
        P("ctx", "tp", None),
        P("ctx", None, "tp"),
        P("ctx", None),
        P("ctx", None),
    )

    return jax.shard_map(
        body, mesh=mesh, in_specs=placed, out_specs=P("ctx", "tp"), check_vma=False
    )
```

profile of v0, /device:TPU:0, one launch (start us, length us, event | category | flops | bytes accessed | tf_op | source)
XLA Modules:
  0.0 220.0 jit_solution(6548665242251781742)
XLA Ops:
  2.0 4.9 %collective-permute-start = (bf16[3,1056]{0,1:T(8,128)(2,1)S(1)}, bf16[3,1056]{0,1:T(8,128)(2,1)S(1)}, u32[]{:S(2)}, u32[]{:S(2)}) collective-permute-start(bf16[3,1056]{0,1:T(8,128)(2,1)S(1)} %fusion.46), channel_id=1, source_target_pairs={{0,4},{4,8},{8,12},{12,16},{16,20},{20,24},{24,28},{1,5},{5,9},{9,... | collective-permute-start | bytes 19016 | tf_op jit(solution)/shard_map/ppermute | solution.py:21
  9.8 2.8 %collective-permute-done = bf16[3,1056]{0,1:T(8,128)(2,1)S(1)} collective-permute-done((bf16[3,1056]{0,1:T(8,128)(2,1)S(1)}, bf16[3,1056]{0,1:T(8,128)(2,1)S(1)}, u32[]{:S(2)}, u32[]{:S(2)}) %collective-permute-start) | collective-permute-done | bytes 6368 | tf_op jit(solution)/shard_map/ppermute | solution.py:21
  12.6 1.5 divide_multiply_fusion
  14.8 7.4 %collective-permute-start.6 = (bf16[17,1024]{1,0:T(8,128)(2,1)S(1)}, bf16[17,1024]{1,0:T(8,128)(2,1)S(1)}, u32[]{:S(2)}, u32[]{:S(2)}) collective-permute-start(bf16[17,1024]{1,0:T(8,128)(2,1)S(1)} %pad_maximum_fusion.3), channel_id=1, source_target_pairs={{0,24},{4,28},{1,25},{5,29},{2,26},{6,30},{3,27},{7,31}} | collective-permute-start | bytes 104456 | tf_op jit(solution)/shard_map/ppermute | solution.py:21
  24.9 2.5 %collective-permute-start.3 = (bf16[17,1024]{1,0:T(8,128)(2,1)S(1)}, bf16[17,1024]{1,0:T(8,128)(2,1)S(1)}, u32[]{:S(2)}, u32[]{:S(2)}) collective-permute-start(bf16[17,1024]{1,0:T(8,128)(2,1)S(1)} %pad_maximum_fusion.3), channel_id=1, source_target_pairs={{0,12},{4,16},{8,20},{12,24},{16,28},{1,13},{5,17},{9,21},{13,25},... | collective-permute-start | bytes 104456 | tf_op jit(solution)/shard_map/ppermute | solution.py:21
  28.7 3.3 %collective-permute-start.1 = (bf16[17,1024]{1,0:T(8,128)(2,1)S(1)}, bf16[17,1024]{1,0:T(8,128)(2,1)S(1)}, u32[]{:S(2)}, u32[]{:S(2)}) collective-permute-start(bf16[17,1024]{1,0:T(8,128)(2,1)S(1)} %pad_maximum_fusion.3), channel_id=1, source_target_pairs={{0,4},{4,8},{8,12},{12,16},{16,20},{20,24},{24,28},{1,5},{5,9},{9,... | collective-permute-start | bytes 104456 | tf_op jit(solution)/shard_map/ppermute | solution.py:21
  33.8 1.6 collective-permute-done.7
  36.5 2.2 %fusion.1 = f32[128,16,64]{0,2,1:T(8,128)S(1)} fusion(f32[128,16,64]{0,2,1:T(8,128)S(1)} %bitcast.57, f32[128,16,64]{0,2,1:T(8,128)S(1)} %bitcast.59, f32[128,128]{1,0:T(8,128)S(1)} %fusion.75, f32[128,16]{0,1:T(8,128)S(1)} %get-tuple-element.15, f32[128,16]{0,1:T(8,128)S(1)} %copy.72, pred[128,128]{1,0:T(8,128)(4,1)S(1)} %iota_compare_fusion.2, ...), kind=kOutput, calls=%fused_computation.11 | convolution fusion | flops 203161600 | bytes 1679424 | tf_op jit(solution)/shard_map/tsh,shp->thp/dot_general | solution.py:74
  39.8 2.2 %collective-permute-start.11 = (bf16[128,1024]{1,0:T(8,128)(2,1)S(1)}, bf16[128,1024]{1,0:T(8,128)(2,1)S(1)}, u32[]{:S(2)}, u32[]{:S(2)}) collective-permute-start(bf16[128,1024]{1,0:T(8,128)(2,1)S(1)} %get-tuple-element.19), channel_id=1, source_target_pairs={{0,16},{4,20},{8,24},{12,28},{16,0},{20,4},{24,8},{28,12},{1,17},{... | collective-permute-start | bytes 786440 | tf_op jit(solution)/shard_map/ppermute | solution.py:30
  42.0 4.0 %collective-permute-start.8 = (bf16[128,1024]{1,0:T(8,128)(2,1)S(1)}, bf16[128,1024]{1,0:T(8,128)(2,1)S(1)}, u32[]{:S(2)}, u32[]{:S(2)}) collective-permute-start(bf16[128,1024]{1,0:T(8,128)(2,1)S(1)} %get-tuple-element.19), channel_id=1, source_target_pairs={{0,4},{4,0},{8,12},{12,8},{16,20},{20,16},{24,28},{28,24},{1,5},{5... | collective-permute-start | bytes 786440 | tf_op jit(solution)/shard_map/ppermute | solution.py:475
  46.7 4.9 %collective-permute-start.14 = (bf16[128,1024]{1,0:T(8,128)(2,1)S(1)}, bf16[128,1024]{1,0:T(8,128)(2,1)S(1)}, u32[]{:S(2)}, u32[]{:S(2)}) collective-permute-start(bf16[128,1024]{1,0:T(8,128)(2,1)S(1)} %collective-permute-done.13), channel_id=1, source_target_pairs={{0,4},{4,0},{8,12},{12,8},{16,20},{20,16},{24,28},{28,24},{1,5},{5... | collective-permute-start | bytes 786440 | tf_op jit(solution)/shard_map/ppermute | solution.py:475
  51.8 10.5 %collective-permute-done.11 = bf16[128,1024]{1,0:T(8,128)(2,1)S(1)} collective-permute-done((bf16[128,1024]{1,0:T(8,128)(2,1)S(1)}, bf16[128,1024]{1,0:T(8,128)(2,1)S(1)}, u32[]{:S(2)}, u32[]{:S(2)}) %collective-permute-start.11) | collective-permute-done | bytes 262176 | tf_op jit(solution)/shard_map/ppermute | solution.py:30
  62.8 1.6 collective-permute-start.10
  64.4 1.7 convolution_bitcast_fusion.3
  66.6 4.0 %collective-permute-done.12 = bf16[128,1024]{1,0:T(8,128)(2,1)S(1)} collective-permute-done((bf16[128,1024]{1,0:T(8,128)(2,1)S(1)}, bf16[128,1024]{1,0:T(8,128)(2,1)S(1)}, u32[]{:S(2)}, u32[]{:S(2)}) %collective-permute-start.12) | collective-permute-done | bytes 262176 | tf_op jit(solution)/shard_map/ppermute | solution.py:475
  71.0 2.4 %collective-permute-done.10 = bf16[128,1024]{1,0:T(8,128)(2,1)S(1)} collective-permute-done((bf16[128,1024]{1,0:T(8,128)(2,1)S(1)}, bf16[128,1024]{1,0:T(8,128)(2,1)S(1)}, u32[]{:S(2)}, u32[]{:S(2)}) %collective-permute-start.10) | collective-permute-done | bytes 262176 | tf_op jit(solution)/shard_map/ppermute | solution.py:475
  76.5 1.5 collective-permute-start.17
  81.2 3.8 %collective-permute-done.17 = bf16[256,512]{1,0:T(8,128)(2,1)S(1)} collective-permute-done((bf16[256,512]{1,0:T(8,128)(2,1)}, bf16[256,512]{1,0:T(8,128)(2,1)S(1)}, u32[]{:S(2)}, u32[]{:S(2)}) %collective-permute-start.17) | collective-permute-done | bytes 262176 | tf_op jit(solution)/shard_map/ppermute | solution.py:25
  86.0 1.8 collective-permute-start.19
  87.9 3.2 %collective-permute-done.19 = bf16[128,512]{1,0:T(8,128)(2,1)S(1)} collective-permute-done((bf16[128,512]{1,0:T(8,128)(2,1)S(1)}, bf16[128,512]{1,0:T(8,128)(2,1)S(1)}, u32[]{:S(2)}, u32[]{:S(2)}) %collective-permute-start.19) | collective-permute-done | bytes 131104 | tf_op jit(solution)/shard_map/ppermute | solution.py:513
  91.4 14.7 %collective-permute-start.24 = (f32[128]{0:T(128)S(1)}, f32[128]{0:T(128)S(1)}, u32[]{:S(2)}, u32[]{:S(2)}) collective-permute-start(f32[128]{0:T(128)S(1)} %fusion.20), channel_id=1, source_target_pairs={{0,2},{1,3},{2,0},{3,1},{4,6},{5,7},{6,4},{7,5},{8,10},{9,11},{10,... | collective-permute-start | bytes 1544 | tf_op jit(solution)/shard_map/ppermute | solution.py:25
  107.6 1.4 collective-permute-done.25
  109.9 108.4 %experts.1 = bf16[128,1024]{1,0:T(8,128)(2,1)} custom-call(bf16[128,1024]{1,0:T(8,128)(2,1)} %fusion.22.expert_input, bf16[288,128]{1,0:T(8,128)(2,1)} %convert_element_type.119.picker, bf16[128,1024]{1,0:T(8,128)(2,1)} %copy-done, bf16[128,288]{1,0:T(8,128)(2,1)} %copy-done.1, bf16[128,288]{1,0:T(8,128)(2,1)} %subtract_convert_fusion.weights_low, ...), custom_call_target="tpu_custom_call" | custom-call | tf_op jit(solution)/shard_map/experts/pallas_call | solution.py:382
  218.3 1.7 copy.89
  (128 shorter events, 25.2 us)
Async XLA Ops:
  2.0 10.6 %collective-permute-start = (bf16[3,1056]{0,1:T(8,128)(2,1)S(1)}, bf16[3,1056]{0,1:T(8,128)(2,1)S(1)}, u32[]{:S(2)}, u32[]{:S(2)}) collective-permute-start(bf16[3,1056]{0,1:T(8,128)(2,1)S(1)} %fusion.46), channel_id=1, source_target_pairs={{0,4},{4,8},{8,12},{12,16},{16,20},{20,24},{24,28},{1,5},{5,9},{9,... | collective-permute-start | bytes 19016 | tf_op jit(solution)/shard_map/ppermute | solution.py:21
  14.8 13.9 %collective-permute-start.6 = (bf16[17,1024]{1,0:T(8,128)(2,1)S(1)}, bf16[17,1024]{1,0:T(8,128)(2,1)S(1)}, u32[]{:S(2)}, u32[]{:S(2)}) collective-permute-start(bf16[17,1024]{1,0:T(8,128)(2,1)S(1)} %pad_maximum_fusion.3), channel_id=1, source_target_pairs={{0,24},{4,28},{1,25},{5,29},{2,26},{6,30},{3,27},{7,31}} | collective-permute-start | bytes 104456 | tf_op jit(solution)/shard_map/ppermute | solution.py:21
  22.3 10.1 %collective-permute-start.5 = (bf16[17,1024]{1,0:T(8,128)(2,1)S(1)}, bf16[17,1024]{1,0:T(8,128)(2,1)S(1)}, u32[]{:S(2)}, u32[]{:S(2)}) collective-permute-start(bf16[17,1024]{1,0:T(8,128)(2,1)S(1)} %pad_maximum_fusion.3), channel_id=1, source_target_pairs={{0,20},{4,24},{8,28},{1,21},{5,25},{9,29},{2,22},{6,26},{10,30},{3... | collective-permute-start | bytes 104456 | tf_op jit(solution)/shard_map/ppermute | solution.py:21
  23.6 10.1 %collective-permute-start.4 = (bf16[17,1024]{1,0:T(8,128)(2,1)S(1)}, bf16[17,1024]{1,0:T(8,128)(2,1)S(1)}, u32[]{:S(2)}, u32[]{:S(2)}) collective-permute-start(bf16[17,1024]{1,0:T(8,128)(2,1)S(1)} %pad_maximum_fusion.3), channel_id=1, source_target_pairs={{0,16},{4,20},{8,24},{12,28},{1,17},{5,21},{9,25},{13,29},{2,18},{... | collective-permute-start | bytes 104456 | tf_op jit(solution)/shard_map/ppermute | solution.py:21
  24.9 8.8 %collective-permute-start.3 = (bf16[17,1024]{1,0:T(8,128)(2,1)S(1)}, bf16[17,1024]{1,0:T(8,128)(2,1)S(1)}, u32[]{:S(2)}, u32[]{:S(2)}) collective-permute-start(bf16[17,1024]{1,0:T(8,128)(2,1)S(1)} %pad_maximum_fusion.3), channel_id=1, source_target_pairs={{0,12},{4,16},{8,20},{12,24},{16,28},{1,13},{5,17},{9,21},{13,25},... | collective-permute-start | bytes 104456 | tf_op jit(solution)/shard_map/ppermute | solution.py:21
  27.4 6.4 %collective-permute-start.2 = (bf16[17,1024]{1,0:T(8,128)(2,1)S(1)}, bf16[17,1024]{1,0:T(8,128)(2,1)S(1)}, u32[]{:S(2)}, u32[]{:S(2)}) collective-permute-start(bf16[17,1024]{1,0:T(8,128)(2,1)S(1)} %pad_maximum_fusion.3), channel_id=1, source_target_pairs={{0,8},{4,12},{8,16},{12,20},{16,24},{20,28},{1,9},{5,13},{9,17},{1... | collective-permute-start | bytes 104456 | tf_op jit(solution)/shard_map/ppermute | solution.py:21
  28.7 5.1 %collective-permute-start.1 = (bf16[17,1024]{1,0:T(8,128)(2,1)S(1)}, bf16[17,1024]{1,0:T(8,128)(2,1)S(1)}, u32[]{:S(2)}, u32[]{:S(2)}) collective-permute-start(bf16[17,1024]{1,0:T(8,128)(2,1)S(1)} %pad_maximum_fusion.3), channel_id=1, source_target_pairs={{0,4},{4,8},{8,12},{12,16},{16,20},{20,24},{24,28},{1,5},{5,9},{9,... | collective-permute-start | bytes 104456 | tf_op jit(solution)/shard_map/ppermute | solution.py:21
  32.4 3.0 %collective-permute-start.7 = (bf16[17,1024]{1,0:T(8,128)(2,1)S(1)}, bf16[17,1024]{1,0:T(8,128)(2,1)S(1)}, u32[]{:S(2)}, u32[]{:S(2)}) collective-permute-start(bf16[17,1024]{1,0:T(8,128)(2,1)S(1)} %pad_maximum_fusion.3), channel_id=1, source_target_pairs={{0,28},{1,29},{2,30},{3,31}} | collective-permute-start | bytes 104456 | tf_op jit(solution)/shard_map/ppermute | solution.py:21
  39.2 7.4 %collective-permute-start.13 = (bf16[128,1024]{1,0:T(8,128)(2,1)S(1)}, bf16[128,1024]{1,0:T(8,128)(2,1)S(1)}, u32[]{:S(2)}, u32[]{:S(2)}) collective-permute-start(bf16[128,1024]{1,0:T(8,128)(2,1)S(1)} %get-tuple-element.19), channel_id=1, source_target_pairs={{0,24},{4,28},{8,0},{12,4},{16,8},{20,12},{24,16},{28,20},{1,25},{... | collective-permute-start | bytes 786440 | tf_op jit(solution)/shard_map/ppermute | solution.py:30
  39.8 22.6 %collective-permute-start.11 = (bf16[128,1024]{1,0:T(8,128)(2,1)S(1)}, bf16[128,1024]{1,0:T(8,128)(2,1)S(1)}, u32[]{:S(2)}, u32[]{:S(2)}) collective-permute-start(bf16[128,1024]{1,0:T(8,128)(2,1)S(1)} %get-tuple-element.19), channel_id=1, source_target_pairs={{0,16},{4,20},{8,24},{12,28},{16,0},{20,4},{24,8},{28,12},{1,17},{... | collective-permute-start | bytes 786440 | tf_op jit(solution)/shard_map/ppermute | solution.py:30
  42.0 20.7 %collective-permute-start.9 = (bf16[128,1024]{1,0:T(8,128)(2,1)S(1)}, bf16[128,1024]{1,0:T(8,128)(2,1)S(1)}, u32[]{:S(2)}, u32[]{:S(2)}) collective-permute-start(bf16[128,1024]{1,0:T(8,128)(2,1)S(1)} %get-tuple-element.19), channel_id=1, source_target_pairs={{0,8},{4,12},{8,16},{12,20},{16,24},{20,28},{24,0},{28,4},{1,9},{5... | collective-permute-start | bytes 786440 | tf_op jit(solution)/shard_map/ppermute | solution.py:30
  42.0 22.4 %collective-permute-start.8 = (bf16[128,1024]{1,0:T(8,128)(2,1)S(1)}, bf16[128,1024]{1,0:T(8,128)(2,1)S(1)}, u32[]{:S(2)}, u32[]{:S(2)}) collective-permute-start(bf16[128,1024]{1,0:T(8,128)(2,1)S(1)} %get-tuple-element.19), channel_id=1, source_target_pairs={{0,4},{4,0},{8,12},{12,8},{16,20},{20,16},{24,28},{28,24},{1,5},{5... | collective-permute-start | bytes 786440 | tf_op jit(solution)/shard_map/ppermute | solution.py:475
  46.7 19.4 %collective-permute-start.14 = (bf16[128,1024]{1,0:T(8,128)(2,1)S(1)}, bf16[128,1024]{1,0:T(8,128)(2,1)S(1)}, u32[]{:S(2)}, u32[]{:S(2)}) collective-permute-start(bf16[128,1024]{1,0:T(8,128)(2,1)S(1)} %collective-permute-done.13), channel_id=1, source_target_pairs={{0,4},{4,0},{8,12},{12,8},{16,20},{20,16},{24,28},{28,24},{1,5},{5... | collective-permute-start | bytes 786440 | tf_op jit(solution)/shard_map/ppermute | solution.py:475
  62.4 8.2 %collective-permute-start.12 = (bf16[128,1024]{1,0:T(8,128)(2,1)S(1)}, bf16[128,1024]{1,0:T(8,128)(2,1)S(1)}, u32[]{:S(2)}, u32[]{:S(2)}) collective-permute-start(bf16[128,1024]{1,0:T(8,128)(2,1)S(1)} %collective-permute-done.11), channel_id=1, source_target_pairs={{0,4},{4,0},{8,12},{12,8},{16,20},{20,16},{24,28},{28,24},{1,5},{5... | collective-permute-start | bytes 786440 | tf_op jit(solution)/shard_map/ppermute | solution.py:475
  62.8 10.6 %collective-permute-start.10 = (bf16[128,1024]{1,0:T(8,128)(2,1)S(1)}, bf16[128,1024]{1,0:T(8,128)(2,1)S(1)}, u32[]{:S(2)}, u32[]{:S(2)}) collective-permute-start(bf16[128,1024]{1,0:T(8,128)(2,1)S(1)} %collective-permute-done.9), channel_id=1, source_target_pairs={{0,4},{4,0},{8,12},{12,8},{16,20},{20,16},{24,28},{28,24},{1,5},{5... | collective-permute-start | bytes 786440 | tf_op jit(solution)/shard_map/ppermute | solution.py:475
  74.8 6.4 %collective-permute-start.15 = (bf16[256,512]{1,0:T(8,128)(2,1)S(1)}, bf16[256,512]{1,0:T(8,128)(2,1)S(1)}, u32[]{:S(2)}, u32[]{:S(2)}) collective-permute-start(bf16[256,512]{1,0:T(8,128)(2,1)S(1)} %get-tuple-element.16), channel_id=1, source_target_pairs={{0,1},{1,0},{2,3},{3,2},{4,5},{5,4},{6,7},{7,6},{8,9},{9,8},{10,11... | collective-permute-start | bytes 786440 | tf_op jit(solution)/shard_map/ppermute | solution.py:25
  76.5 8.6 %collective-permute-start.17 = (bf16[256,512]{1,0:T(8,128)(2,1)}, bf16[256,512]{1,0:T(8,128)(2,1)S(1)}, u32[]{:S(2)}, u32[]{:S(2)}) collective-permute-start(bf16[256,512]{1,0:T(8,128)(2,1)} %fusion.35), channel_id=1, source_target_pairs={{0,2},{1,3},{2,0},{3,1},{4,6},{5,7},{6,4},{7,5},{8,10},{9,11},{10,... | collective-permute-start | bytes 786440 | tf_op jit(solution)/shard_map/ppermute | solution.py:25
  79.0 8.8 %collective-permute-start.21 = (f32[128]{0:T(128)S(1)}, f32[128]{0:T(128)S(1)}, u32[]{:S(2)}, u32[]{:S(2)}) collective-permute-start(f32[128]{0:T(128)S(1)} %get-tuple-element.18), channel_id=1, source_target_pairs={{0,2},{1,3},{2,0},{3,1},{4,6},{5,7},{6,4},{7,5},{8,10},{9,11},{10,... | collective-permute-start | bytes 1544 | tf_op jit(solution)/shard_map/ppermute | solution.py:25
  79.6 8.3 %collective-permute-start.22 = (f32[128]{0:T(128)S(1)}, f32[128]{0:T(128)S(1)}, u32[]{:S(2)}, u32[]{:S(2)}) collective-permute-start(f32[128]{0:T(128)S(1)} %get-tuple-element.18), channel_id=1, source_target_pairs={{0,3},{1,2},{2,1},{3,0},{4,7},{5,6},{6,5},{7,4},{8,11},{9,10},{10,... | collective-permute-start | bytes 1544 | tf_op jit(solution)/shard_map/ppermute | solution.py:25
  80.3 7.6 %collective-permute-start.20 = (f32[128]{0:T(128)S(1)}, f32[128]{0:T(128)S(1)}, u32[]{:S(2)}, u32[]{:S(2)}) collective-permute-start(f32[128]{0:T(128)S(1)} %get-tuple-element.18), channel_id=1, source_target_pairs={{0,1},{1,0},{2,3},{3,2},{4,5},{5,4},{6,7},{7,6},{8,9},{9,8},{10,11... | collective-permute-start | bytes 1544 | tf_op jit(solution)/shard_map/ppermute | solution.py:25
  86.0 5.0 %collective-permute-start.19 = (bf16[128,512]{1,0:T(8,128)(2,1)S(1)}, bf16[128,512]{1,0:T(8,128)(2,1)S(1)}, u32[]{:S(2)}, u32[]{:S(2)}) collective-permute-start(bf16[128,512]{1,0:T(8,128)(2,1)S(1)} %get-tuple-element.25), channel_id=1, source_target_pairs={{0,4},{1,12},{2,20},{3,28},{4,0},{5,8},{6,16},{7,24},{8,5},{9,13},... | collective-permute-start | bytes 393224 | tf_op jit(solution)/shard_map/ppermute | solution.py:513
  91.4 16.2 %collective-permute-start.24 = (f32[128]{0:T(128)S(1)}, f32[128]{0:T(128)S(1)}, u32[]{:S(2)}, u32[]{:S(2)}) collective-permute-start(f32[128]{0:T(128)S(1)} %fusion.20), channel_id=1, source_target_pairs={{0,2},{1,3},{2,0},{3,1},{4,6},{5,7},{6,4},{7,5},{8,10},{9,11},{10,... | collective-permute-start | bytes 1544 | tf_op jit(solution)/shard_map/ppermute | solution.py:25
  106.1 3.0 %collective-permute-start.25 = (f32[128]{0:T(128)S(1)}, f32[128]{0:T(128)S(1)}, u32[]{:S(2)}, u32[]{:S(2)}) collective-permute-start(f32[128]{0:T(128)S(1)} %fusion.20), channel_id=1, source_target_pairs={{0,3},{1,2},{2,1},{3,0},{4,7},{5,6},{6,5},{7,4},{8,11},{9,10},{10,... | collective-permute-start | bytes 1544 | tf_op jit(solution)/shard_map/ppermute | solution.py:25
  106.1 3.0 %collective-permute-start.23 = (f32[128]{0:T(128)S(1)}, f32[128]{0:T(128)S(1)}, u32[]{:S(2)}, u32[]{:S(2)}) collective-permute-start(f32[128]{0:T(128)S(1)} %fusion.20), channel_id=1, source_target_pairs={{0,1},{1,0},{2,3},{3,2},{4,5},{5,4},{6,7},{7,6},{8,9},{9,8},{10,11... | collective-permute-start | bytes 1544 | tf_op jit(solution)/shard_map/ppermute | solution.py:25
  (16 other events, 193.6 us)
where the time goes:
time: 221 us; the launch traced here: 220 us
  Pallas kernels  108 us (49%)
  starting transfers between devices  58 us (26%)
  waiting for transfers between devices  31.1 us (14%)
  other arithmetic  8.98 us (4%)
  matrix products  7.04 us (3%)
  local copies, waits for them, and re-layouts  5.62 us (3%)
    pallas_call x1, Pallas kernels, experts_direct(): pl.pallas_call(functools.partial(expert_kernel, peers), out_shape=jax.Sha...  108 us
    ppermute x8, starting transfers between devices, passed_along(): lax.ppermute(value, axis, [(source, source + steps) for source in range(f...  23.3 us
    ppermute x9, starting transfers between devices, swapped(): lax.ppermute(value, 'tp', [(p, p ^ distance) for p in range(lax.axis_size...  18.9 us
    ppermute x4, starting transfers between devices, body(): lax.ppermute(block, 'ctx', [(c, c ^ 1) for c in range(context_count)])  10.9 us
    ppermute x3, waiting for transfers between devices, rotated(): lax.ppermute(value, 'ctx', [(c, (c + steps) % count) for c in range(count)])  10.6 us
    ppermute x9, waiting for transfers between devices, swapped(): lax.ppermute(value, 'tp', [(p, p ^ distance) for p in range(lax.axis_size...  6.6 us
    ppermute x4, waiting for transfers between devices, body(): lax.ppermute(block, 'ctx', [(c, c ^ 1) for c in range(context_count)])  6.35 us
  transfers between devices with their start and end apart: 26, of which 11 were waited for; matrix products, arithmetic and copies ran while one was open for 5% of the time, Pallas kernels for 0%

commit v1 on v0

--- a/solution.py
+++ b/solution.py
@@ -107,17 +107,25 @@
     return (i == j * fold + part).astype(jnp.bfloat16)
 
 
-def expert_kernel(
+def block_kernel(
     peers,
-    expert_input,
+    gated,
+    mixer_gain,
+    residual,
+    feed_gain,
     picker,
-    hidden,
     weights_high,
     weights_low,
+    weight_own,
+    weight_beyond,
     gate,
     up,
     down,
     out,
+    hidden,
+    expert_input,
+    stats,
+    stats_in,
     gate_tiles,
     up_tiles,
     down_tiles,
@@ -138,6 +146,14 @@
     active_diagonal,
     total,
     tile_sem,
+    weight_sem,
+    line_send,
+    line_receive,
+    merge_send,
+    merge_receive,
+    final_receive,
+    stats_send,
+    stats_receive,
     home_send,
     home_receive,
     pair_send,
@@ -172,9 +188,23 @@
 
         lax.fori_loop(0, chunks, body, 0)
 
+    z, x = ctx // 2, ctx % 2
+    core, side = tp % 2, tp // 2
+    line = peers // 2
+    tokens = residual.shape[0]
+    half = tokens // 2
+    held = down_tiles.at[3]
+
+    def weight_copy(n):
+        source = (weight_own, weight_beyond)[n // 2].at[:, pl.ds(n % 2 * CHUNK, CHUNK)]
+        place = 2 * (x if n < 2 else 1 - x) + n % 2
+        return pltpu.make_async_copy(source, gate_tiles.at[3, place], weight_sem.at[n])
+
+    for n in range(4):
+        weight_copy(n).start()
     start_group([(kind, place) for place in (0, 1) for kind in (0, 1)])
-    start_group([(kind, place) for place in (2, 3) for kind in (0, 1)])
-    start_group([(2, place) for place in range(4)])
+    start_group([(0, 2), (1, 2), (1, 3)])
+    start_group([(2, place) for place in range(3)])
 
     barrier = pltpu.get_barrier_semaphore()
     for distance in range(1, peers):
@@ -183,6 +213,174 @@
         )
     for other in (beside, across, diagonal):
         pl.semaphore_signal(barrier, inc=1, device_id={"tp": other}, device_id_type=MESH)
+
+    @pl.when(z != tp)
+    def _():
+        pl.semaphore_signal(
+            barrier, inc=1, device_id={"ctx": tp * 2 + x, "tp": beside}, device_id_type=MESH
+        )
+
+    def piece_of(b, h):
+        return held.at[b // 2, pl.ds(pl.multiple_of(b % 2 * tokens + h * half, half), half), :]
+
+    def slab(kind, b):
+        return held.at[line // 2 + kind, pl.ds(pl.multiple_of(b * half, half), half), :]
+
+    def as_row(column):
+        return jnp.broadcast_to(column, (tokens, tokens)).T[:8]
+
+    def as_column(row):
+        return jnp.broadcast_to(row[:1], (tokens, tokens)).T[:, :1]
+
+    def stats_copy(kind, n):
+        other = (beside, across, diagonal)[n]
+        return remote(
+            stats.at[kind], stats_in.at[kind, n], stats_send.at[kind, n], stats_receive.at[kind, n], {"tp": other}
+        )
+
+    def stats_total(kind):
+        for n in range(3):
+            stats_copy(kind, n).wait_recv()
+        row = (stats[kind] + stats_in[kind, 0]) + (stats_in[kind, 1] + stats_in[kind, 2])
+        return lax.rsqrt(as_column(row) / (width * 4) + EPSILON)
+
+    value = gated[...]
+    held[z // 2, pl.ds(pl.multiple_of(z % 2 * tokens, tokens), tokens), :] = (
+        value * mixer_gain[...]
+    ).astype(jnp.bfloat16)
+    stats[0] = as_row(jnp.sum(value * value, axis=1, keepdims=True))
+    pl.semaphore_wait(barrier, peers - 1 + 3 + jnp.where(z == beside, line - 1, 0))
+
+    def line_copy(direction, b, h):
+        return remote(
+            piece_of(b, h),
+            piece_of(b, h),
+            line_send.at[direction, b, h],
+            line_receive.at[b, h],
+            {"ctx": (ctx + 2 - 4 * direction + peers) % peers},
+        )
+
+    for h in range(2):
+
+        @pl.when(z < line - 1)
+        def _():
+            line_copy(0, z, h).start()
+
+        @pl.when(z > 0)
+        def _():
+            line_copy(1, z, h).start()
+
+    for n in range(3):
+        stats_copy(0, n).start()
+    for n in range(4):
+        weight_copy(n).wait()
+
+    def give_copy(b):
+        return remote(slab(0, b), slab(1, b), merge_send.at[0, b], merge_receive.at[0, b], {"tp": beside})
+
+    def cross_copy(b):
+        return remote(slab(2, b), slab(3, b), merge_send.at[1, b], merge_receive.at[1, b], {"tp": across})
+
+    def final_copy(b):
+        return remote(
+            slab(2, b),
+            slab(4, core),
+            merge_send.at[1, b],
+            final_receive.at[core],
+            {"ctx": b * 2 + x, "tp": z},
+        )
+
+    def mine(slot):
+        return pl.ds(pl.multiple_of(slot * tokens + core * half, half), half)
+
+    def store(kind, b, data):
+        held[line // 2 + kind, pl.ds(pl.multiple_of(b * half, half), half), :] = data
+
+    def forward(b, direction):
+        for h in range(2):
+            line_copy(direction, b, h).wait_recv()
+
+            @pl.when((z < line - 1) if direction == 0 else (z > 0))
+            def _():
+                line_copy(direction, b, h).start()
+
+    def multiply(b, slot):
+        block = held[b // 2, pl.ds(pl.multiple_of(b % 2 * tokens, tokens), tokens), :]
+        for n in range(4):
+            total[slot * tokens : (slot + 1) * tokens, n * CHUNK : (n + 1) * CHUNK] = jnp.dot(
+                block, gate_tiles[3, n], preferred_element_type=jnp.float32
+            )
+        theirs = pl.ds(pl.multiple_of(slot * tokens + (1 - core) * half, half), half)
+        store(0, b, total[theirs, :].astype(jnp.bfloat16))
+        give_copy(b).start()
+
+    def merge(b, slot):
+        give_copy(b).wait_recv()
+        joint = total[mine(slot), :] + slab(1, b)[...].astype(jnp.float32)
+
+        @pl.when(side != z // 2)
+        def _():
+            store(2, b, joint.astype(jnp.bfloat16))
+            cross_copy(b).start()
+
+        @pl.when(side == z // 2)
+        def _():
+            total[mine(slot), :] = joint
+
+    def deliver(b, slot):
+        @pl.when(side == z // 2)
+        def _():
+            cross_copy(b).wait_recv()
+            joint = (total[mine(slot), :] + slab(3, b)[...].astype(jnp.float32)).astype(jnp.bfloat16)
+            stays = jnp.logical_and(b == z, tp == z)
+
+            @pl.when(stays)
+            def _():
+                store(4, core, joint)
+
+            @pl.when(jnp.logical_not(stays))
+            def _():
+                store(2, b, joint)
+                final_copy(b).start()
+
+    def each(step, action):
+        if step == 0:
+            action(z, 0)
+            return
+
+        @pl.when(z - step >= 0)
+        def _():
+            action(z - step, 0)
+
+        @pl.when(z + step < line)
+        def _():
+            action(z + step, 1)
+
+    for step in range(line):
+        if step > 0:
+            each(step, forward)
+            each(step - 1, deliver)
+        each(step, multiply)
+        each(step, merge)
+    each(line - 1, deliver)
+
+    scale = stats_total(0)
+    for h in range(2):
+
+        @pl.when(jnp.logical_not(jnp.logical_and(z == tp, core == h)))
+        def _():
+            remote(
+                slab(4, h), slab(4, h), merge_send.at[1, 0], final_receive.at[h], {"tp": beside}
+            ).wait_recv()
+
+    mixer_out = held[line // 2 + 4, :tokens, :].astype(jnp.float32) * scale
+    hidden[...] = (residual[...].astype(jnp.float32) + mixer_out).astype(jnp.bfloat16)
+    state = hidden[...].astype(jnp.float32)
+    stats[1] = as_row(jnp.sum(state * state, axis=1, keepdims=True))
+    for n in range(3):
+        stats_copy(1, n).start()
+    feed_scale = stats_total(1)
+    expert_input[...] = (state * feed_scale * feed_gain[...]).astype(jnp.bfloat16)
 
     picked = jnp.dot(picker[...], expert_input[...], preferred_element_type=jnp.float32)
     packed[...] = picked[: peers * main].astype(jnp.bfloat16)
@@ -195,7 +393,6 @@
             preferred_element_type=jnp.float32,
         )
     packed_extra[...] = folded.astype(jnp.bfloat16)
-    pl.semaphore_wait(barrier, peers - 1 + 3)
 
     def travel(sources, targets, sign, base):
         copies = []
@@ -219,6 +416,34 @@
         copy.start()
     rows[:main] = packed[:main]
     rows_extra[:SUB] = packed_extra[:SUB]
+    for kind in range(2):
+        for n in range(3):
+            stats_copy(kind, n).wait_send()
+    for b in range(line):
+
+        @pl.when(jnp.logical_and(z < line - 1, b <= z))
+        def _():
+            for h in range(2):
+                line_copy(0, b, h).wait_send()
+
+        @pl.when(jnp.logical_and(z > 0, b >= z))
+        def _():
+            for h in range(2):
+                line_copy(1, b, h).wait_send()
+
+        give_copy(b).wait_send()
+
+        @pl.when(side != z // 2)
+        def _():
+            cross_copy(b).wait_send()
+
+        @pl.when(
+            jnp.logical_and(side == z // 2, jnp.logical_not(jnp.logical_and(z == b, tp == z)))
+        )
+        def _():
+            final_copy(b).wait_send()
+
+    start_group([(0, 3), (2, 3)])
     for copy in outward:
         copy.wait_recv()
     landed = rows_extra[...]
@@ -352,10 +577,12 @@
         copy.wait_send()
 
 
-def experts_direct(expert_input, hidden, expert_ids, expert_weights, gate, up, down):
+def block_direct(
+    gated, mixer_gain, residual, feed_gain, weights_out, expert_ids, expert_weights, gate, up, down
+):
     peers = lax.axis_size("ctx")
     ctx = lax.axis_index("ctx")
-    tokens, width = expert_input.shape
+    tokens, width = residual.shape
     hidden_width = gate.shape[2] // 4
     chunks = hidden_width // CHUNK
     main = CAP // SUB * SUB
@@ -380,11 +607,15 @@
     block = (chunks, count, CHUNK)
     low = jnp.bfloat16
     return pl.pallas_call(
-        functools.partial(expert_kernel, peers),
+        functools.partial(block_kernel, peers),
         out_shape=jax.ShapeDtypeStruct((tokens, width), low),
-        in_specs=[vmem] * 5 + [anywhere] * 3,
+        in_specs=[vmem] * 7 + [anywhere] * 5,
         out_specs=vmem,
         scratch_shapes=[
+            pltpu.VMEM((tokens, width), low),
+            pltpu.VMEM((tokens, width), low),
+            pltpu.VMEM((2, 8, tokens), jnp.float32),
+            pltpu.VMEM((2, 3, 8, tokens), jnp.float32),
             pltpu.VMEM((4, chunks, width, CHUNK), low),
             pltpu.VMEM((4, chunks, width, CHUNK), low),
             pltpu.VMEM((4, chunks, CHUNK, width), low),
@@ -405,6 +636,14 @@
             pltpu.VMEM(block, low),
             pltpu.VMEM((count, width), jnp.float32),
             pltpu.SemaphoreType.DMA((12, chunks)),
+            pltpu.SemaphoreType.DMA((4,)),
+            pltpu.SemaphoreType.DMA((2, peers // 2, 2)),
+            pltpu.SemaphoreType.DMA((peers // 2, 2)),
+            pltpu.SemaphoreType.DMA((2, peers // 2)),
+            pltpu.SemaphoreType.DMA((2, peers // 2)),
+            pltpu.SemaphoreType.DMA((2,)),
+            pltpu.SemaphoreType.DMA((2, 3)),
+            pltpu.SemaphoreType.DMA((2, 3)),
             pltpu.SemaphoreType.DMA((4, peers)),
             pltpu.SemaphoreType.DMA((4, peers)),
             pltpu.SemaphoreType.DMA((9, chunks)),
@@ -413,8 +652,21 @@
         compiler_params=pltpu.CompilerParams(
             collective_id=0, has_side_effects=True, vmem_limit_bytes=66_000_000
         ),
-        name="experts",
-    )(expert_input, picker, hidden, weights_high, weights_low, gate, up, down)
+        name="block",
+    )(
+        gated,
+        mixer_gain[None, :],
+        residual,
+        feed_gain[None, :],
+        picker,
+        weights_high,
+        weights_low,
+        weights_out[0],
+        weights_out[1],
+        gate,
+        up,
+        down,
+    )
 
 
 def body(
@@ -445,6 +697,9 @@
     heads_local = step_raw.shape[1]
     head_size = channels // heads_local
     taps = conv_weight.shape[0]
+    direct = context_count == EXPERTS
+    if direct:
+        weight_beyond = lax.ppermute(out_weight, "ctx", [(c, c ^ 1) for c in range(context_count)])
     joined = jnp.concatenate([mixer_input, state_proj], axis=1)
     previous = passed_along(joined[tokens - (taps - 1) :], "ctx", 1)
     kernel = jnp.concatenate([conv_weight, conv_state_weight], axis=1)
@@ -463,10 +718,22 @@
     )
     mixed = inside + carried + skip_gain[None, :, None] * values
     gated = mixed.reshape(tokens, channels) * jax.nn.silu(gate_input.astype(jnp.float32))
+    if direct:
+        return block_direct(
+            gated,
+            mixer_gain,
+            residual,
+            feed_gain,
+            (out_weight, weight_beyond),
+            expert_ids,
+            expert_weights,
+            expert_gate,
+            expert_up,
+            expert_down,
+        )
     tp_index = lax.axis_index("tp")
     core, chip = (tp_index % 2, tp_index // 2)
     scaled = (gated * mixer_gain[None, :]).astype(jnp.bfloat16)
-    direct = context_count == EXPERTS
     ctx_index = lax.axis_index("ctx")
     if direct:
         pairs = []
@@ -527,10 +794,6 @@
     feed_sum = tensor_total(jnp.sum(state_float * state_float, axis=1))
     feed_scale = lax.rsqrt(feed_sum / width_total + EPSILON)
     expert_input = (state_float * feed_scale[:, None] * feed_gain[None, :]).astype(jnp.bfloat16)
-    if direct:
-        return experts_direct(
-            expert_input, hidden_state, expert_ids, expert_weights, expert_gate, expert_up, expert_down
-        )
     group = context_count // EXPERTS
     width_local = expert_input.shape[1]
     flat_experts = expert_ids.reshape(-1)

time: 221 us -> 190 us (0.86)
  Pallas kernels: 108 us -> 144 us
  starting transfers between devices: 58 us -> 22.6 us
  waiting for transfers between devices: 31.1 us -> 1.63 us
  matrix products: 7.04 us -> 4.72 us
    pallas_call x1, Pallas kernels: 108 us -> 144 us  [block_direct(): pl.pallas_call(functools.partial(block_kernel, peers), out_shape=jax.Shap...]
    ppermute x18 -> x1, starting transfers between devices: 34.7 us -> 1.6 us  [body(): lax.ppermute(out_weight, 'ctx', [(c, c ^ 1) for c in range(context_count)])]
    ppermute x18 -> x1, waiting for transfers between devices: 26.7 us -> 0.01 us  [body(): lax.ppermute(out_weight, 'ctx', [(c, c ^ 1) for c in range(context_count)])]
    dot_general x4 -> x0, matrix products: 2.98 us -> none  [body(): pairs.append(jnp.dot(pair, out_weight, preferred_element_type=jnp.float32))]
    ppermute x8, waiting for transfers between devices: 4.39 us -> 1.62 us  [passed_along(): lax.ppermute(value, axis, [(source, source + steps) for source in range(f...]
    ppermute x8, starting transfers between devices: 23.3 us -> 21 us  [passed_along(): lax.ppermute(value, axis, [(source, source + steps) for source in range(f...]
  transfers between devices with their start and end apart: 26 -> 9, of which waited for: 11 -> 1; matrix products, arithmetic and copies ran while one was open for 5% -> 9% of each run, Pallas kernels for 0% -> 0%
where the time goes in v1:
time: 190 us
  Pallas kernels  144 us (76%)
  starting transfers between devices  22.6 us (12%)
  other arithmetic  8.85 us (5%)
  local copies, waits for them, and re-layouts  7.3 us (4%)
  matrix products  4.72 us (2%)
    pallas_call x1, Pallas kernels, block_direct(): pl.pallas_call(functools.partial(block_kernel, peers), out_shape=jax.Shap...  144 us
    ppermute x8, starting transfers between devices, passed_along(): lax.ppermute(value, axis, [(source, source + steps) for source in range(f...  21 us
    unnamed x8, local copies, waits for them, and re-layouts  4.35 us
  transfers between devices with their start and end apart: 9, of which 1 were waited for; matrix products, arithmetic and copies ran while one was open for 9% of the time, Pallas kernels for 0%

profile of v1, /device:TPU:0, one launch (start us, length us, event | category | flops | bytes accessed | tf_op | source)
XLA Modules:
  0.0 189.8 jit_solution(8297032349185533130)
XLA Ops:
  0.0 1.2 copy.70
  1.2 0.8 fusion.28
  2.0 4.9 %collective-permute-start = (bf16[3,1056]{0,1:T(8,128)(2,1)S(1)}, bf16[3,1056]{0,1:T(8,128)(2,1)S(1)}, u32[]{:S(2)}, u32[]{:S(2)}) collective-permute-start(bf16[3,1056]{0,1:T(8,128)(2,1)S(1)} %fusion.28), channel_id=1, source_target_pairs={{0,4},{4,8},{8,12},{12,16},{16,20},{20,24},{24,28},{1,5},{5,9},{9,... | collective-permute-start | bytes 19016 | tf_op jit(solution)/shard_map/ppermute | solution.py:21
  6.9 1.6 collective-permute-start.8
  9.2 0.8 negate_multiply_fusion
  10.3 0.8 fusion.27
  11.1 0.8 copy.78
  13.3 0.7 compare_select_fusion.3
  14.1 0.7 select_reduce_fusion
  14.9 0.7 constant_dynamic-update-slice_fusion.1
  17.5 1.5 divide_multiply_fusion
  19.6 4.0 %collective-permute-start.6 = (bf16[17,1024]{1,0:T(8,128)(2,1)S(1)}, bf16[17,1024]{1,0:T(8,128)(2,1)S(1)}, u32[]{:S(2)}, u32[]{:S(2)}) collective-permute-start(bf16[17,1024]{1,0:T(8,128)(2,1)S(1)} %pad_maximum_fusion.2), channel_id=1, source_target_pairs={{0,24},{4,28},{1,25},{5,29},{2,26},{6,30},{3,27},{7,31}} | collective-permute-start | bytes 104456 | tf_op jit(solution)/shard_map/ppermute | solution.py:21
  23.6 1.3 collective-permute-start.5
  25.7 1.3 collective-permute-start.4
  27.0 3.9 %collective-permute-start.3 = (bf16[17,1024]{1,0:T(8,128)(2,1)S(1)}, bf16[17,1024]{1,0:T(8,128)(2,1)S(1)}, u32[]{:S(2)}, u32[]{:S(2)}) collective-permute-start(bf16[17,1024]{1,0:T(8,128)(2,1)S(1)} %pad_maximum_fusion.2), channel_id=1, source_target_pairs={{0,12},{4,16},{8,20},{12,24},{16,28},{1,13},{5,17},{9,21},{13,25},... | collective-permute-start | bytes 104456 | tf_op jit(solution)/shard_map/ppermute | solution.py:21
  30.9 1.3 collective-permute-start.2
  32.2 3.1 %collective-permute-start.1 = (bf16[17,1024]{1,0:T(8,128)(2,1)S(1)}, bf16[17,1024]{1,0:T(8,128)(2,1)S(1)}, u32[]{:S(2)}, u32[]{:S(2)}) collective-permute-start(bf16[17,1024]{1,0:T(8,128)(2,1)S(1)} %pad_maximum_fusion.2), channel_id=1, source_target_pairs={{0,4},{4,8},{8,12},{12,16},{16,20},{20,24},{24,28},{1,5},{5,9},{9,... | collective-permute-start | bytes 104456 | tf_op jit(solution)/shard_map/ppermute | solution.py:21
  35.7 1.3 collective-permute-start.7
  37.1 1.6 collective-permute-done.7
  38.7 1.0 fusion.31
  39.7 2.9 %fusion.1 = f32[128,16,64]{0,2,1:T(8,128)S(1)} fusion(f32[128,16,64]{0,2,1:T(8,128)S(1)} %bitcast.33, f32[128,16,64]{0,2,1:T(8,128)S(1)} %bitcast.35, f32[128,128]{1,0:T(8,128)S(1)} %fusion.55, f32[128,16]{0,1:T(8,128)S(1)} %get-tuple-element.15, f32[128,16]{0,1:T(8,128)S(1)} %copy.72, pred[128,128]{1,0:T(8,128)(4,1)S(1)} %iota_compare_fusion.2, ...), kind=kOutput, calls=%fused_computation.6 | convolution fusion | flops 203161600 | bytes 1679424 | tf_op jit(solution)/shard_map/tsh,shp->thp/dot_general | solution.py:74
  42.8 1.0 fusion.19.gated
  43.8 144.3 %block.1 = bf16[128,1024]{1,0:T(8,128)(2,1)} custom-call(f32[128,1024]{1,0:T(8,128)} %fusion.19.gated, f32[1,1024]{1,0:T(1,128)} %bitcast.42, bf16[128,1024]{1,0:T(8,128)(2,1)} %residual.1, f32[1,1024]{1,0:T(1,128)} %bitcast.43, bf16[288,128]{1,0:T(8,128)(2,1)} %convert_element_type.59.picker, bf16[128,288]{1,0:T(8,128)(2,1)} %copy-done, ...), custom_call_target="tpu_custom_call" | custom-call | tf_op jit(solution)/shard_map/block/pallas_call | solution.py:609
  188.1 1.7 copy.89
  (56 shorter events, 6.4 us)
Async XLA Ops:
  0.0 42.8 %copy-start.1 = (bf16[128,1024]{1,0:T(8,128)(2,1)S(1)}, bf16[128,1024]{1,0:T(8,128)(2,1)}, u32[]{:S(2)}) copy-start(bf16[128,1024]{1,0:T(8,128)(2,1)} %param.20) | copy-start | bytes 786436
  2.0 15.4 %collective-permute-start = (bf16[3,1056]{0,1:T(8,128)(2,1)S(1)}, bf16[3,1056]{0,1:T(8,128)(2,1)S(1)}, u32[]{:S(2)}, u32[]{:S(2)}) collective-permute-start(bf16[3,1056]{0,1:T(8,128)(2,1)S(1)} %fusion.28), channel_id=1, source_target_pairs={{0,4},{4,8},{8,12},{12,16},{16,20},{20,24},{24,28},{1,5},{5,9},{9,... | collective-permute-start | bytes 19016 | tf_op jit(solution)/shard_map/ppermute | solution.py:21
  6.9 36.9 %collective-permute-start.8 = (bf16[1024,512]{1,0:T(8,128)(2,1)}, bf16[1024,512]{1,0:T(8,128)(2,1)}, u32[]{:S(2)}, u32[]{:S(2)}) collective-permute-start(bf16[1024,512]{1,0:T(8,128)(2,1)} %weight_own.1), channel_id=1, source_target_pairs={{0,4},{4,0},{8,12},{12,8},{16,20},{20,16},{24,28},{28,24},{1,5},{5... | collective-permute-start | bytes 3145736 | tf_op jit(solution)/shard_map/ppermute | solution.py:702
  15.8 28.0 %copy-start = (bf16[128,288]{1,0:T(8,128)(2,1)}, bf16[128,288]{1,0:T(8,128)(2,1)S(1)}, u32[]{:S(2)}) copy-start(bf16[128,288]{1,0:T(8,128)(2,1)S(1)} %copy.85.weights_high) | copy-start | bytes 221188
  19.6 11.3 %collective-permute-start.6 = (bf16[17,1024]{1,0:T(8,128)(2,1)S(1)}, bf16[17,1024]{1,0:T(8,128)(2,1)S(1)}, u32[]{:S(2)}, u32[]{:S(2)}) collective-permute-start(bf16[17,1024]{1,0:T(8,128)(2,1)S(1)} %pad_maximum_fusion.2), channel_id=1, source_target_pairs={{0,24},{4,28},{1,25},{5,29},{2,26},{6,30},{3,27},{7,31}} | collective-permute-start | bytes 104456 | tf_op jit(solution)/shard_map/ppermute | solution.py:21
  23.6 8.6 %collective-permute-start.5 = (bf16[17,1024]{1,0:T(8,128)(2,1)S(1)}, bf16[17,1024]{1,0:T(8,128)(2,1)S(1)}, u32[]{:S(2)}, u32[]{:S(2)}) collective-permute-start(bf16[17,1024]{1,0:T(8,128)(2,1)S(1)} %pad_maximum_fusion.2), channel_id=1, source_target_pairs={{0,20},{4,24},{8,28},{1,21},{5,25},{9,29},{2,22},{6,26},{10,30},{3... | collective-permute-start | bytes 104456 | tf_op jit(solution)/shard_map/ppermute | solution.py:21
  25.7 10.0 %collective-permute-start.4 = (bf16[17,1024]{1,0:T(8,128)(2,1)S(1)}, bf16[17,1024]{1,0:T(8,128)(2,1)S(1)}, u32[]{:S(2)}, u32[]{:S(2)}) collective-permute-start(bf16[17,1024]{1,0:T(8,128)(2,1)S(1)} %pad_maximum_fusion.2), channel_id=1, source_target_pairs={{0,16},{4,20},{8,24},{12,28},{1,17},{5,21},{9,25},{13,29},{2,18},{... | collective-permute-start | bytes 104456 | tf_op jit(solution)/shard_map/ppermute | solution.py:21
  27.0 10.0 %collective-permute-start.3 = (bf16[17,1024]{1,0:T(8,128)(2,1)S(1)}, bf16[17,1024]{1,0:T(8,128)(2,1)S(1)}, u32[]{:S(2)}, u32[]{:S(2)}) collective-permute-start(bf16[17,1024]{1,0:T(8,128)(2,1)S(1)} %pad_maximum_fusion.2), channel_id=1, source_target_pairs={{0,12},{4,16},{8,20},{12,24},{16,28},{1,13},{5,17},{9,21},{13,25},... | collective-permute-start | bytes 104456 | tf_op jit(solution)/shard_map/ppermute | solution.py:21
  30.9 6.1 %collective-permute-start.2 = (bf16[17,1024]{1,0:T(8,128)(2,1)S(1)}, bf16[17,1024]{1,0:T(8,128)(2,1)S(1)}, u32[]{:S(2)}, u32[]{:S(2)}) collective-permute-start(bf16[17,1024]{1,0:T(8,128)(2,1)S(1)} %pad_maximum_fusion.2), channel_id=1, source_target_pairs={{0,8},{4,12},{8,16},{12,20},{16,24},{20,28},{1,9},{5,13},{9,17},{1... | collective-permute-start | bytes 104456 | tf_op jit(solution)/shard_map/ppermute | solution.py:21
  32.2 4.8 %collective-permute-start.1 = (bf16[17,1024]{1,0:T(8,128)(2,1)S(1)}, bf16[17,1024]{1,0:T(8,128)(2,1)S(1)}, u32[]{:S(2)}, u32[]{:S(2)}) collective-permute-start(bf16[17,1024]{1,0:T(8,128)(2,1)S(1)} %pad_maximum_fusion.2), channel_id=1, source_target_pairs={{0,4},{4,8},{8,12},{12,16},{16,20},{20,24},{24,28},{1,5},{5,9},{9,... | collective-permute-start | bytes 104456 | tf_op jit(solution)/shard_map/ppermute | solution.py:21
  35.7 3.0 %collective-permute-start.7 = (bf16[17,1024]{1,0:T(8,128)(2,1)S(1)}, bf16[17,1024]{1,0:T(8,128)(2,1)S(1)}, u32[]{:S(2)}, u32[]{:S(2)}) collective-permute-start(bf16[17,1024]{1,0:T(8,128)(2,1)S(1)} %pad_maximum_fusion.2), channel_id=1, source_target_pairs={{0,28},{1,29},{2,30},{3,31}} | collective-permute-start | bytes 104456 | tf_op jit(solution)/shard_map/ppermute | solution.py:21

commit v2 on v1

--- a/solution.py
+++ b/solution.py
@@ -109,15 +109,21 @@
 
 def block_kernel(
     peers,
-    gated,
+    mixer_input,
+    gate_input,
+    state_proj,
+    step_raw,
+    conv_weight,
+    conv_state_weight,
+    step_bias,
+    decay_log,
+    skip_gain,
     mixer_gain,
     residual,
     feed_gain,
-    picker,
-    weights_high,
-    weights_low,
+    expert_ids,
+    expert_weights,
     weight_own,
-    weight_beyond,
     gate,
     up,
     down,
@@ -126,6 +132,22 @@
     expert_input,
     stats,
     stats_in,
+    picker,
+    weights_high,
+    weights_low,
+    edge_in,
+    edge_state,
+    edge_state_in,
+    states_long,
+    wide_state,
+    wide_sums,
+    wide_step,
+    state_out,
+    state_in,
+    tail_out,
+    tail_in,
+    entering_state,
+    logs,
     gate_tiles,
     up_tiles,
     down_tiles,
@@ -147,6 +169,12 @@
     total,
     tile_sem,
     weight_sem,
+    weight_send,
+    weight_receive,
+    edge_send,
+    edge_receive,
+    state_send,
+    state_receive,
     line_send,
     line_receive,
     merge_send,
@@ -196,11 +224,26 @@
     held = down_tiles.at[3]
 
     def weight_copy(n):
-        source = (weight_own, weight_beyond)[n // 2].at[:, pl.ds(n % 2 * CHUNK, CHUNK)]
-        place = 2 * (x if n < 2 else 1 - x) + n % 2
-        return pltpu.make_async_copy(source, gate_tiles.at[3, place], weight_sem.at[n])
-
-    for n in range(4):
+        source = weight_own.at[:, pl.ds(n * CHUNK, CHUNK)]
+        return pltpu.make_async_copy(source, gate_tiles.at[3, 2 * x + n], weight_sem.at[n])
+
+    def weight_across(n):
+        span = pl.ds(n // 2 * CHUNK, CHUNK)
+        return remote(
+            weight_own.at[span, pl.ds(n % 2 * CHUNK, CHUNK)],
+            gate_tiles.at[3, 2 * x + n % 2, span, :],
+            weight_send.at[n],
+            weight_receive.at[n],
+            {"ctx": ctx + 1 - 2 * x},
+        )
+
+    pieces = 2 * width // CHUNK
+    for distance in range(peers):
+        state_in[distance] = jnp.zeros(state_in.shape[1:], state_in.dtype)
+        tail_in[distance] = jnp.zeros(tail_in.shape[1:], tail_in.dtype)
+    edge_state[...] = jnp.zeros_like(edge_state)
+    edge_state[:, : state_proj.shape[1]] = state_proj[tokens - SUB :, :]
+    for n in range(2):
         weight_copy(n).start()
     start_group([(kind, place) for place in (0, 1) for kind in (0, 1)])
     start_group([(0, 2), (1, 2), (1, 3)])
@@ -244,12 +287,189 @@
         row = (stats[kind] + stats_in[kind, 0]) + (stats_in[kind, 1] + stats_in[kind, 2])
         return lax.rsqrt(as_column(row) / (width * 4) + EPSILON)
 
-    value = gated[...]
-    held[z // 2, pl.ds(pl.multiple_of(z % 2 * tokens, tokens), tokens), :] = (
-        value * mixer_gain[...]
+    lanes = tokens
+    states = state_proj.shape[1] // 2
+    heads = step_raw.shape[1]
+    slabs = width // lanes
+    values = total.at[pl.ds(tokens + SUB, tokens)]
+    exact = lax.Precision.HIGHEST
+    total[8 : 8 + tokens, :] = mixer_input[...].astype(jnp.float32)
+    states_long[8 : 8 + tokens, :] = state_proj[...].astype(jnp.float32)
+    step_size = jax.nn.softplus(step_raw[...] + step_bias[...])
+    log_decay = -step_size * jnp.exp(decay_log[...])
+    row_index = lax.broadcasted_iota(jnp.int32, (tokens, tokens), 0)
+    column_index = lax.broadcasted_iota(jnp.int32, (tokens, tokens), 1)
+    causal = row_index >= column_index
+    cumulative = jnp.dot(
+        causal.astype(jnp.float32), log_decay, precision=exact, preferred_element_type=jnp.float32
+    )
+    wide_sums[...] = jnp.zeros_like(wide_sums)
+    wide_step[...] = jnp.zeros_like(wide_step)
+    wide_state[...] = jnp.zeros_like(wide_state)
+    wide_sums[:, :heads] = cumulative
+    wide_step[:, :heads] = step_size
+    sums_row, step_row = wide_sums[...].T, wide_step[...].T
+    tail_out[...] = jnp.broadcast_to(wide_sums[tokens - 1 :, :], tail_out.shape)
+
+    kinds = lax.broadcasted_iota(jnp.int32, (tokens, EXPERTS), 1)
+    named = [(expert_ids[:, k : k + 1] == kinds).astype(jnp.float32) for k in range(2)]
+    before = jnp.dot(
+        (row_index > column_index).astype(jnp.bfloat16),
+        (named[0] + named[1]).astype(jnp.bfloat16),
+        preferred_element_type=jnp.float32,
+    )
+    relative = ((kinds - ctx + peers) % peers).astype(jnp.float32)
+    spots = jnp.where(
+        before < main, relative * main + before, peers * main + relative * extra + before - main
+    )
+    targets = [jnp.sum(named[k] * spots, axis=1, keepdims=True) for k in range(2)]
+    slot_row = lax.broadcasted_iota(jnp.int32, picker.shape, 0).astype(jnp.float32)
+    slot_column = lax.broadcasted_iota(jnp.int32, weights_high.shape, 1).astype(jnp.float32)
+    picked_rows = [as_row(target)[:1] for target in targets]
+    picker[...] = (
+        jnp.where(slot_row == picked_rows[0], 1.0, 0.0) + jnp.where(slot_row == picked_rows[1], 1.0, 0.0)
     ).astype(jnp.bfloat16)
-    stats[0] = as_row(jnp.sum(value * value, axis=1, keepdims=True))
+    weights = jnp.where(slot_column == targets[0], expert_weights[:, 0:1], 0.0)
+    weights = weights + jnp.where(slot_column == targets[1], expert_weights[:, 1:2], 0.0)
+    high = weights.astype(jnp.bfloat16)
+    weights_high[...] = high
+    weights_low[...] = (weights - high.astype(jnp.float32)).astype(jnp.bfloat16)
+
     pl.semaphore_wait(barrier, peers - 1 + 3 + jnp.where(z == beside, line - 1, 0))
+
+    def edge_copies():
+        device = {"ctx": (ctx + 1) % peers}
+        return (
+            remote(
+                mixer_input.at[pl.ds(tokens - SUB, SUB), :], edge_in, edge_send.at[0], edge_receive.at[0], device
+            ),
+            remote(edge_state, edge_state_in, edge_send.at[1], edge_receive.at[1], device),
+        )
+
+    @pl.when(ctx < peers - 1)
+    def _():
+        for copy in edge_copies():
+            copy.start()
+
+    for n in range(2):
+        weight_across(n).start()
+
+    @pl.when(ctx > 0)
+    def _():
+        for copy in edge_copies():
+            copy.wait_recv()
+        total[:8, :] = edge_in[...].astype(jnp.float32)[8:]
+        states_long[:8, :] = edge_state_in[...].astype(jnp.float32)[8:, : 2 * states]
+
+    @pl.when(ctx == 0)
+    def _():
+        total[:8, :] = jnp.zeros((8, width), jnp.float32)
+        states_long[:8, :] = jnp.zeros((8, 2 * states), jnp.float32)
+
+    taps = conv_weight.shape[0]
+    base = 8 - (taps - 1)
+    filtered = jnp.zeros((tokens, 2 * states), jnp.float32)
+    for tap in range(taps):
+        filtered = filtered + conv_state_weight[tap : tap + 1, :] * states_long[base + tap : base + tap + tokens, :]
+    wide_state[:, : 2 * states] = jax.nn.silu(filtered)
+    state_rows = wide_state[...].T
+    writer_rows = state_rows[:states]
+    ending = jnp.exp(wide_sums[tokens - 1 :, :] - wide_sums[...]) * wide_step[...]
+    left = lax.broadcasted_iota(jnp.int32, (tokens, lanes), 1) < lanes // 2
+
+    def widened(narrow, i):
+        return jnp.where(left, narrow[:, 2 * i : 2 * i + 1], narrow[:, 2 * i + 1 : 2 * i + 2])
+
+    for i in range(slabs):
+        slab_of = slice(i * lanes, (i + 1) * lanes)
+        value = jnp.zeros((tokens, lanes), jnp.float32)
+        for tap in range(taps):
+            value = value + conv_weight[tap : tap + 1, slab_of] * total[base + tap : base + tap + tokens, slab_of]
+        value = jax.nn.silu(value)
+        values[:, slab_of] = value
+        state_out[:, slab_of] = jnp.dot(
+            writer_rows, widened(ending, i) * value, precision=exact, preferred_element_type=jnp.float32
+        ).astype(jnp.bfloat16)
+
+    def state_copies(distance):
+        device = {"ctx": (ctx + distance) % peers}
+        return (
+            remote(
+                state_out, state_in.at[distance], state_send.at[0, distance], state_receive.at[0, distance], device
+            ),
+            remote(
+                tail_out, tail_in.at[distance], state_send.at[1, distance], state_receive.at[1, distance], device
+            ),
+        )
+
+    for distance in range(peers - 1, 0, -1):
+
+        @pl.when(ctx + distance < peers)
+        def _():
+            for copy in state_copies(distance):
+                copy.start()
+
+    for n in range(2, pieces):
+        weight_across(n).start()
+    scores = jnp.dot(
+        wide_state[:, states : 2 * states], writer_rows, precision=exact, preferred_element_type=jnp.float32
+    )
+    for i in range(slabs):
+        slab_of = slice(i * lanes, (i + 1) * lanes)
+        factors = []
+        for head in (2 * i, 2 * i + 1):
+            spans = wide_sums[:, head : head + 1] - sums_row[head : head + 1, :]
+            factors.append(
+                jnp.exp(jnp.where(causal, spans, -1e30)) * (step_row[head : head + 1, :] * scores)
+            )
+        value = values[:, slab_of]
+        halves = jnp.concatenate([jnp.where(left, value, 0.0), jnp.where(left, 0.0, value)], axis=0)
+        inside = jnp.dot(
+            jnp.concatenate(factors, axis=1).astype(jnp.bfloat16),
+            halves.astype(jnp.bfloat16),
+            preferred_element_type=jnp.float32,
+        )
+        total[:tokens, slab_of] = inside + widened(skip_gain, i) * value
+
+    for distance in range(1, peers):
+
+        @pl.when(ctx - distance >= 0)
+        def _():
+            for copy in state_copies(distance):
+                copy.wait_recv()
+
+    logs[...] = jnp.zeros_like(logs)
+    running = jnp.zeros((1, tokens), jnp.float32)
+    for distance in range(1, peers):
+        logs[distance - 1 : distance, :] = running
+        running = running + tail_in[distance][:1]
+    spread = (
+        lax.broadcasted_iota(jnp.int32, (lanes, width), 1) // (width // heads)
+        == lax.broadcasted_iota(jnp.int32, (lanes, width), 0)
+    ).astype(jnp.float32)
+    carries = jnp.dot(jnp.exp(logs[...]), spread, precision=exact, preferred_element_type=jnp.float32)
+    arrived = jnp.zeros((states, width), jnp.float32)
+    for distance in range(1, peers):
+        arrived = arrived + carries[distance - 1 : distance, :] * state_in[distance].astype(jnp.float32)
+    entering_state[:states, :] = jnp.zeros((states, width), jnp.float32)
+    entering_state[states:, :] = arrived
+    growth = jnp.exp(wide_sums[...])
+    squares = jnp.zeros((tokens, lanes), jnp.float32)
+    for i in range(slabs):
+        slab_of = slice(i * lanes, (i + 1) * lanes)
+        carried = jnp.dot(
+            wide_state[:, : 2 * states],
+            entering_state[:, slab_of],
+            precision=exact,
+            preferred_element_type=jnp.float32,
+        )
+        mixed = total[:tokens, slab_of] + carried * widened(growth, i)
+        value = mixed * jax.nn.silu(gate_input[:, slab_of].astype(jnp.float32))
+        squares = squares + value * value
+        held[z // 2, pl.ds(pl.multiple_of(z % 2 * tokens, tokens), tokens), slab_of] = (
+            value * mixer_gain[:, slab_of]
+        ).astype(jnp.bfloat16)
+    stats[0] = as_row(jnp.sum(squares, axis=1, keepdims=True))
 
     def line_copy(direction, b, h):
         return remote(
@@ -272,8 +492,10 @@
 
     for n in range(3):
         stats_copy(0, n).start()
-    for n in range(4):
+    for n in range(2):
         weight_copy(n).wait()
+    for n in range(pieces):
+        weight_across(n).wait_recv()
 
     def give_copy(b):
         return remote(slab(0, b), slab(1, b), merge_send.at[0, b], merge_receive.at[0, b], {"tp": beside})
@@ -419,6 +641,21 @@
     for kind in range(2):
         for n in range(3):
             stats_copy(kind, n).wait_send()
+    for n in range(pieces):
+        weight_across(n).wait_send()
+
+    @pl.when(ctx < peers - 1)
+    def _():
+        for copy in edge_copies():
+            copy.wait_send()
+
+    for distance in range(1, peers):
+
+        @pl.when(ctx + distance < peers)
+        def _():
+            for copy in state_copies(distance):
+                copy.wait_send()
+
     for b in range(line):
 
         @pl.when(jnp.logical_and(z < line - 1, b <= z))
@@ -578,30 +815,32 @@
 
 
 def block_direct(
-    gated, mixer_gain, residual, feed_gain, weights_out, expert_ids, expert_weights, gate, up, down
+    residual,
+    mixer_input,
+    gate_input,
+    state_proj,
+    step_raw,
+    conv_weight,
+    conv_state_weight,
+    step_bias,
+    decay_log,
+    skip_gain,
+    mixer_gain,
+    out_weight,
+    feed_gain,
+    gate,
+    up,
+    down,
+    expert_ids,
+    expert_weights,
 ):
     peers = lax.axis_size("ctx")
-    ctx = lax.axis_index("ctx")
     tokens, width = residual.shape
-    hidden_width = gate.shape[2] // 4
-    chunks = hidden_width // CHUNK
-    main = CAP // SUB * SUB
-    extra = CAP - main
+    states = state_proj.shape[1] // 2
+    chunks = gate.shape[2] // 4 // CHUNK
+    extra = CAP - CAP // SUB * SUB
+    main = CAP - extra
     count = peers * CAP
-    flat = expert_ids.reshape(-1)
-    matches = (flat[:, None] == jnp.arange(EXPERTS)[None, :]).astype(jnp.int32)
-    slots = jnp.sum((jnp.cumsum(matches, axis=0) - matches) * matches, axis=1)
-    places = (flat - ctx) % EXPERTS
-    targets = jnp.where(
-        slots < main, places * main + slots, peers * main + places * extra + slots - main
-    ).reshape(tokens, -1)
-    chosen = targets[:, :, None] == jnp.arange(count)[None, None, :]
-    weights = jnp.sum(jnp.where(chosen, expert_weights[:, :, None], 0.0), axis=1)
-    weights_high = weights.astype(jnp.bfloat16)
-    weights_low = (weights - weights_high.astype(jnp.float32)).astype(jnp.bfloat16)
-    picker = jnp.any(
-        targets[None, :, :] == jnp.arange(count)[:, None, None], axis=2
-    ).astype(jnp.bfloat16)
     vmem = pl.BlockSpec(memory_space=pltpu.VMEM)
     anywhere = pl.BlockSpec(memory_space=pl.ANY)
     block = (chunks, count, CHUNK)
@@ -609,13 +848,29 @@
     return pl.pallas_call(
         functools.partial(block_kernel, peers),
         out_shape=jax.ShapeDtypeStruct((tokens, width), low),
-        in_specs=[vmem] * 7 + [anywhere] * 5,
+        in_specs=[vmem] * 14 + [anywhere] * 4,
         out_specs=vmem,
         scratch_shapes=[
             pltpu.VMEM((tokens, width), low),
             pltpu.VMEM((tokens, width), low),
             pltpu.VMEM((2, 8, tokens), jnp.float32),
             pltpu.VMEM((2, 3, 8, tokens), jnp.float32),
+            pltpu.VMEM((count, tokens), low),
+            pltpu.VMEM((tokens, count), low),
+            pltpu.VMEM((tokens, count), low),
+            pltpu.VMEM((SUB, width), low),
+            pltpu.VMEM((SUB, tokens), low),
+            pltpu.VMEM((SUB, tokens), low),
+            pltpu.VMEM((8 + tokens, 2 * states), jnp.float32),
+            pltpu.VMEM((tokens, tokens), jnp.float32),
+            pltpu.VMEM((tokens, tokens), jnp.float32),
+            pltpu.VMEM((tokens, tokens), jnp.float32),
+            pltpu.VMEM((states, width), low),
+            pltpu.VMEM((peers, states, width), low),
+            pltpu.VMEM((8, tokens), jnp.float32),
+            pltpu.VMEM((peers, 8, tokens), jnp.float32),
+            pltpu.VMEM((2 * states, width), jnp.float32),
+            pltpu.VMEM((8, tokens), jnp.float32),
             pltpu.VMEM((4, chunks, width, CHUNK), low),
             pltpu.VMEM((4, chunks, width, CHUNK), low),
             pltpu.VMEM((4, chunks, CHUNK, width), low),
@@ -636,7 +891,13 @@
             pltpu.VMEM(block, low),
             pltpu.VMEM((count, width), jnp.float32),
             pltpu.SemaphoreType.DMA((12, chunks)),
-            pltpu.SemaphoreType.DMA((4,)),
+            pltpu.SemaphoreType.DMA((2,)),
+            pltpu.SemaphoreType.DMA((2 * width // CHUNK,)),
+            pltpu.SemaphoreType.DMA((2 * width // CHUNK,)),
+            pltpu.SemaphoreType.DMA((2,)),
+            pltpu.SemaphoreType.DMA((2,)),
+            pltpu.SemaphoreType.DMA((2, peers)),
+            pltpu.SemaphoreType.DMA((2, peers)),
             pltpu.SemaphoreType.DMA((2, peers // 2, 2)),
             pltpu.SemaphoreType.DMA((peers // 2, 2)),
             pltpu.SemaphoreType.DMA((2, peers // 2)),
@@ -654,15 +915,21 @@
         ),
         name="block",
     )(
-        gated,
+        mixer_input,
+        gate_input,
+        state_proj,
+        step_raw,
+        conv_weight,
+        conv_state_weight,
+        step_bias[None, :],
+        decay_log[None, :],
+        skip_gain[None, :],
         mixer_gain[None, :],
         residual,
         feed_gain[None, :],
-        picker,
-        weights_high,
-        weights_low,
-        weights_out[0],
-        weights_out[1],
+        expert_ids,
+        expert_weights,
+        out_weight,
         gate,
         up,
         down,
@@ -698,8 +965,6 @@
     head_size = channels // heads_local
     taps = conv_weight.shape[0]
     direct = context_count == EXPERTS
-    if direct:
-        weight_beyond = lax.ppermute(out_weight, "ctx", [(c, c ^ 1) for c in range(context_count)])
     joined = jnp.concatenate([mixer_input, state_proj], axis=1)
     previous = passed_along(joined[tokens - (taps - 1) :], "ctx", 1)
     kernel = jnp.concatenate([conv_weight, conv_state_weight], axis=1)
@@ -718,19 +983,6 @@
     )
     mixed = inside + carried + skip_gain[None, :, None] * values
     gated = mixed.reshape(tokens, channels) * jax.nn.silu(gate_input.astype(jnp.float32))
-    if direct:
-        return block_direct(
-            gated,
-            mixer_gain,
-            residual,
-            feed_gain,
-            (out_weight, weight_beyond),
-            expert_ids,
-            expert_weights,
-            expert_gate,
-            expert_up,
-            expert_down,
-        )
     tp_index = lax.axis_index("tp")
     core, chip = (tp_index % 2, tp_index // 2)
     scaled = (gated * mixer_gain[None, :]).astype(jnp.bfloat16)
@@ -892,6 +1144,11 @@
         P("ctx", None),
     )
 
+    direct = mesh.shape["ctx"] == EXPERTS and mesh.shape["tp"] == 4
+
+    def layer(*args):
+        return (block_direct if direct else body)(*args)
+
     return jax.shard_map(
-        body, mesh=mesh, in_specs=placed, out_specs=P("ctx", "tp"), check_vma=False
+        layer, mesh=mesh, in_specs=placed, out_specs=P("ctx", "tp"), check_vma=False
     )

time: 190 us -> 175 us (0.921)
  Pallas kernels: 144 us -> 168 us
  starting transfers between devices: 22.6 us -> 0 us
  other arithmetic: 8.85 us -> 0 us
  matrix products: 4.72 us -> 0 us
    pallas_call x1, Pallas kernels: 144 us -> 168 us  [block_direct(): pl.pallas_call(functools.partial(block_kernel, peers), out_shape=jax.Shap...]
    ppermute x9 -> x0, starting transfers between devices: 22.6 us -> none  [the longest x8 21 us: passed_along(): lax.ppermute(value, axis, [(source, source + steps) for source in range(f...]
    dot_general x4 -> x0, matrix products: 4.72 us -> none  [the longest x1 2.9 us: local_terms(): jnp.einsum('tsh,shp->thp', factor, values, precision=lax.Precision.HIGHEST)]
    mul x6 -> x0, other arithmetic: 3.42 us -> none  [the longest x1 1.49 us: causal_filter(): return jax.nn.silu(total)]
    unnamed x8 -> x5, local copies, waits for them, and re-layouts: 4.35 us -> 7.3 us
    convert_element_type x12 -> x0, other arithmetic: 2.19 us -> none  [the longest x1 0.76 us: body(): joined.astype(jnp.float32)]
  transfers between devices with their start and end apart: 9 -> 0, of which waited for: 1 -> 0; matrix products, arithmetic and copies ran while one was open for 9% -> 0% of each run, Pallas kernels for 0% -> 0%
where the time goes in v2:
time: 175 us
  Pallas kernels  168 us (96%)
  local copies, waits for them, and re-layouts  7.3 us (4%)
    pallas_call x1, Pallas kernels, block_direct(): pl.pallas_call(functools.partial(block_kernel, peers), out_shape=jax.Shap...  168 us
    unnamed x5, local copies, waits for them, and re-layouts  7.3 us

profile of v2, /device:TPU:0, one launch (start us, length us, event | category | flops | bytes accessed | tf_op | source)
XLA Modules:
  0.0 174.9 jit_solution(6537300309915668243)
XLA Ops:
  0.0 1.4 copy.19.state_proj
  1.4 1.4 copy.20.step_raw
  2.8 1.4 copy.21.expert_ids
  4.2 1.4 copy.22.expert_weights
  5.6 167.6 %block.1 = bf16[128,1024]{1,0:T(8,128)(2,1)} custom-call(bf16[128,1024]{1,0:T(8,128)(2,1)} %mixer_input.1, bf16[128,1024]{1,0:T(8,128)(2,1)} %gate_input.1, bf16[128,32]{1,0:T(8,128)(2,1)} %copy.19.state_proj, f32[128,16]{1,0:T(8,128)} %copy.20.step_raw, f32[4,1024]{1,0:T(4,128)} %conv_weight.1, f32[4,32]{1,0:T(4,128)} %conv_state_weight.1, ...), custom_call_target="tpu_custom_call" | custom-call | tf_op jit(solution)/shard_map/block/pallas_call | solution.py:848
  173.3 1.7 copy.24

commit v3 on v2

--- a/solution.py
+++ b/solution.py
@@ -192,10 +192,12 @@
     across = (tp + 2) % 4
     diagonal = 3 - tp
     width = rows.shape[1]
-    chunks = first.shape[1]
+    chunks = first.shape[2]
     hidden_width = chunks * CHUNK
     main = packed.shape[0] // peers
     extra = (rows.shape[0] - peers * main) // peers
+    near = peers // 2
+    group = near * (main + extra)
     fold = SUB // extra
     piece = width // fold
 
@@ -241,8 +243,12 @@
     for distance in range(peers):
         state_in[distance] = jnp.zeros(state_in.shape[1:], state_in.dtype)
         tail_in[distance] = jnp.zeros(tail_in.shape[1:], tail_in.dtype)
-    edge_state[...] = jnp.zeros_like(edge_state)
-    edge_state[:, : state_proj.shape[1]] = state_proj[tokens - SUB :, :]
+    states = state_proj.shape[0] // 2
+    heads = step_raw.shape[0]
+    wide_state[...] = jnp.zeros_like(wide_state)
+    wide_state[: 2 * states, :] = state_proj[...].astype(jnp.float32)
+    state_columns = wide_state[...].T
+    edge_state[...] = state_columns[tokens - SUB :].astype(jnp.bfloat16)
     for n in range(2):
         weight_copy(n).start()
     start_group([(kind, place) for place in (0, 1) for kind in (0, 1)])
@@ -288,14 +294,18 @@
         return lax.rsqrt(as_column(row) / (width * 4) + EPSILON)
 
     lanes = tokens
-    states = state_proj.shape[1] // 2
-    heads = step_raw.shape[1]
     slabs = width // lanes
     values = total.at[pl.ds(tokens + SUB, tokens)]
     exact = lax.Precision.HIGHEST
     total[8 : 8 + tokens, :] = mixer_input[...].astype(jnp.float32)
-    states_long[8 : 8 + tokens, :] = state_proj[...].astype(jnp.float32)
-    step_size = jax.nn.softplus(step_raw[...] + step_bias[...])
+    states_long[8 : 8 + tokens, :] = state_columns[:, : 2 * states]
+    wide_step[...] = jnp.zeros_like(wide_step)
+    wide_step[:heads, :] = step_raw[...]
+    step_size = jax.nn.softplus(wide_step[...].T[:, :heads] + step_bias[...])
+    wide_sums[...] = jnp.zeros_like(wide_sums)
+    wide_sums[:2, :] = expert_ids[...].astype(jnp.float32)
+    wide_sums[2:4, :] = expert_weights[...]
+    route = wide_sums[...].T
     log_decay = -step_size * jnp.exp(decay_log[...])
     row_index = lax.broadcasted_iota(jnp.int32, (tokens, tokens), 0)
     column_index = lax.broadcasted_iota(jnp.int32, (tokens, tokens), 1)
@@ -312,15 +322,17 @@
     tail_out[...] = jnp.broadcast_to(wide_sums[tokens - 1 :, :], tail_out.shape)
 
     kinds = lax.broadcasted_iota(jnp.int32, (tokens, EXPERTS), 1)
-    named = [(expert_ids[:, k : k + 1] == kinds).astype(jnp.float32) for k in range(2)]
+    named = [(route[:, k : k + 1] == kinds.astype(jnp.float32)).astype(jnp.float32) for k in range(2)]
     before = jnp.dot(
         (row_index > column_index).astype(jnp.bfloat16),
         (named[0] + named[1]).astype(jnp.bfloat16),
         preferred_element_type=jnp.float32,
     )
-    relative = ((kinds - ctx + peers) % peers).astype(jnp.float32)
-    spots = jnp.where(
-        before < main, relative * main + before, peers * main + relative * extra + before - main
+    relative = kinds ^ ctx
+    start = (relative // near * group).astype(jnp.float32)
+    inner = (relative % near).astype(jnp.float32)
+    spots = start + jnp.where(
+        before < main, inner * main + before, near * main + inner * extra + before - main
     )
     targets = [jnp.sum(named[k] * spots, axis=1, keepdims=True) for k in range(2)]
     slot_row = lax.broadcasted_iota(jnp.int32, picker.shape, 0).astype(jnp.float32)
@@ -329,8 +341,8 @@
     picker[...] = (
         jnp.where(slot_row == picked_rows[0], 1.0, 0.0) + jnp.where(slot_row == picked_rows[1], 1.0, 0.0)
     ).astype(jnp.bfloat16)
-    weights = jnp.where(slot_column == targets[0], expert_weights[:, 0:1], 0.0)
-    weights = weights + jnp.where(slot_column == targets[1], expert_weights[:, 1:2], 0.0)
+    weights = jnp.where(slot_column == targets[0], route[:, 2:3], 0.0)
+    weights = weights + jnp.where(slot_column == targets[1], route[:, 3:4], 0.0)
     high = weights.astype(jnp.bfloat16)
     weights_high[...] = high
     weights_low[...] = (weights - high.astype(jnp.float32)).astype(jnp.bfloat16)
@@ -604,38 +616,64 @@
     feed_scale = stats_total(1)
     expert_input[...] = (state * feed_scale * feed_gain[...]).astype(jnp.bfloat16)
 
-    picked = jnp.dot(picker[...], expert_input[...], preferred_element_type=jnp.float32)
-    packed[...] = picked[: peers * main].astype(jnp.bfloat16)
-    tail = picked[peers * main :].astype(jnp.bfloat16)
-    folded = jnp.zeros((peers * SUB, piece), jnp.float32)
-    for part in range(fold):
-        folded = folded + jnp.dot(
-            refold(peers, extra, fold, part),
-            tail[:, part * piece : (part + 1) * piece],
-            preferred_element_type=jnp.float32,
-        )
-    packed_extra[...] = folded.astype(jnp.bfloat16)
-
-    def travel(sources, targets, sign, base):
+    def pack(g, block):
+        packed[g * near * main : (g + 1) * near * main, :] = block[: near * main].astype(jnp.bfloat16)
+        tail = block[near * main :].astype(jnp.bfloat16)
+        folded = jnp.zeros((near * SUB, piece), jnp.float32)
+        for part in range(fold):
+            folded = folded + jnp.dot(
+                refold(near, extra, fold, part),
+                tail[:, part * piece : (part + 1) * piece],
+                preferred_element_type=jnp.float32,
+            )
+        packed_extra[g * near * SUB : (g + 1) * near * SUB, :] = folded.astype(jnp.bfloat16)
+
+    def unpack(g, target, landed):
+        block = landed[g * near * SUB : (g + 1) * near * SUB, :]
+        for part in range(fold):
+            target[g * group + near * main : (g + 1) * group, part * piece : (part + 1) * piece] = jnp.dot(
+                unfold(near, extra, fold, part), block, preferred_element_type=jnp.float32
+            ).astype(jnp.bfloat16)
+
+    def partner(r):
+        high = (ctx // 4 + r // 4) % 2
+        middle = (ctx // 2 % 2 + r // 2 % 2) % 2
+        return {"ctx": 4 * high + 2 * middle + (ctx % 2 + r % 2) % 2}
+
+    def travel(g, target, target_extra, kind):
         copies = []
-        for kind, (source, target) in enumerate(zip(sources, targets)):
-            size = (main, SUB)[kind]
-            for distance in range(1, peers):
-                block = pl.ds(distance * size, size)
-                copies.append(
-                    remote(
-                        source.at[block],
-                        target.at[block],
-                        home_send.at[base + kind, distance],
-                        home_receive.at[base + kind, distance],
-                        {"ctx": (ctx + sign * distance + peers) % peers},
-                    )
+        for r in range(max(1, g * near), (g + 1) * near):
+            spot = pl.ds(g * group + r % near * main, main)
+            tile_rows = pl.ds(r * SUB, SUB)
+            copies.append(
+                remote(
+                    packed.at[pl.ds(r * main, main)],
+                    target.at[spot],
+                    home_send.at[kind, r],
+                    home_receive.at[kind, r],
+                    partner(r),
                 )
+            )
+            copies.append(
+                remote(
+                    packed_extra.at[tile_rows],
+                    target_extra.at[tile_rows],
+                    home_send.at[kind + 1, r],
+                    home_receive.at[kind + 1, r],
+                    partner(r),
+                )
+            )
         return copies
 
-    outward = travel((packed, packed_extra), (rows, rows_extra), 1, 0)
-    for copy in outward:
-        copy.start()
+    for g in range(2):
+        pack(
+            g,
+            jnp.dot(
+                picker[g * group : (g + 1) * group, :], expert_input[...], preferred_element_type=jnp.float32
+            ),
+        )
+        for copy in travel(g, rows, rows_extra, 0):
+            copy.start()
     rows[:main] = packed[:main]
     rows_extra[:SUB] = packed_extra[:SUB]
     for kind in range(2):
@@ -681,137 +719,147 @@
             final_copy(b).wait_send()
 
     start_group([(0, 3), (2, 3)])
-    for copy in outward:
-        copy.wait_recv()
-    landed = rows_extra[...]
-    for part in range(fold):
-        rows[peers * main :, part * piece : (part + 1) * piece] = jnp.dot(
-            unfold(peers, extra, fold, part), landed, preferred_element_type=jnp.float32
-        ).astype(jnp.bfloat16)
-
-    def pair(kind, j, source, target, other):
-        return remote(source, target, pair_send.at[kind, j], pair_receive.at[kind, j], {"tp": other})
+
+    def pair(g, kind, j, source, target, other):
+        return remote(source, target, pair_send.at[g, kind, j], pair_receive.at[g, kind, j], {"tp": other})
 
     both = (gate_tiles, up_tiles)
 
-    def product(which, place, j):
-        tile(which, place, j).wait()
-        return jnp.dot(rows[...], both[which][place, j], preferred_element_type=jnp.float32)
-
-    def first_copy(which, j):
-        return pair(which, j, first.at[which, j], first_in.at[which, j], beside)
-
-    def far_copy(which, j):
-        return pair(2 + which, j, far.at[which, j], far_in.at[which, j], across)
-
-    def near_copy(which, j):
-        return pair(4 + which, j, first.at[which, j], near_in.at[which, j], beside)
-
-    def beside_copy(j):
-        return pair(6, j, active.at[j], active_beside.at[j], beside)
-
-    def across_copy(j):
-        return pair(7, j, active.at[j], active_across.at[j], across)
-
-    def diagonal_copy(j):
-        return pair(8, j, active_across.at[j], active_diagonal.at[j], beside)
-
-    def far_step(j, carry):
+    def product(g, which, place, j, fresh):
+        if fresh:
+            tile(which, place, j).wait()
+        return jnp.dot(
+            rows[g * group : (g + 1) * group, :], both[which][place, j], preferred_element_type=jnp.float32
+        )
+
+    def first_copy(g, which, j):
+        return pair(g, which, j, first.at[g, which, j], first_in.at[g, which, j], beside)
+
+    def far_copy(g, which, j):
+        return pair(g, 2 + which, j, far.at[g, which, j], far_in.at[g, which, j], across)
+
+    def near_copy(g, which, j):
+        return pair(g, 4 + which, j, first.at[g, which, j], near_in.at[g, which, j], beside)
+
+    def beside_copy(g, j):
+        return pair(g, 6, j, active.at[g, j], active_beside.at[g, j], beside)
+
+    def across_copy(g, j):
+        return pair(g, 7, j, active.at[g, j], active_across.at[g, j], across)
+
+    def diagonal_copy(g, j):
+        return pair(g, 8, j, active_across.at[g, j], active_diagonal.at[g, j], beside)
+
+    def loop(step):
+        def run(j, carry):
+            step(j)
+            return carry
+
+        lax.fori_loop(0, chunks, run, 0)
+
+    def receive_rows(g):
+        for copy in travel(g, rows, rows_extra, 0):
+            copy.wait_recv()
+        unpack(g, rows, rows_extra)
+
+    def far_step(g, fresh, j):
         for which in range(2):
-            first[which, j] = product(which, 0, j).astype(jnp.bfloat16)
-            first_copy(which, j).start()
+            first[g, which, j] = product(g, which, 0, j, fresh).astype(jnp.bfloat16)
+            first_copy(g, which, j).start()
         for which in range(2):
-            mine = product(which, 1, j)
-            first_copy(which, j).wait_recv()
-            far[which, j] = (mine + first_in[which, j].astype(jnp.float32)).astype(jnp.bfloat16)
-            far_copy(which, j).start()
-        return carry
-
-    lax.fori_loop(0, chunks, far_step, 0)
-
-    def near_step(j, carry):
+            mine = product(g, which, 1, j, fresh)
+            first_copy(g, which, j).wait_recv()
+            far[g, which, j] = (mine + first_in[g, which, j].astype(jnp.float32)).astype(jnp.bfloat16)
+            far_copy(g, which, j).start()
+
+    def near_step(g, fresh, j):
         for which in range(2):
-            mine = product(which, 2, j).astype(jnp.bfloat16)
-            first_copy(which, j).wait_send()
-            first[which, j] = mine
-            near_copy(which, j).start()
-        return carry
-
-    lax.fori_loop(0, chunks, near_step, 0)
-    total[...] = jnp.zeros_like(total)
-
-    def lowered(source, place, j):
-        tile(2, place, j).wait()
-        total[...] += jnp.dot(source[j], down_tiles[place, j], preferred_element_type=jnp.float32)
-
-    def own_step(j, carry):
+            mine = product(g, which, 2, j, fresh).astype(jnp.bfloat16)
+            first_copy(g, which, j).wait_send()
+            first[g, which, j] = mine
+            near_copy(g, which, j).start()
+
+    def lowered(g, source, place, j, fresh):
+        if fresh:
+            tile(2, place, j).wait()
+        total[g * group : (g + 1) * group, :] += jnp.dot(
+            source[g, j], down_tiles[place, j], preferred_element_type=jnp.float32
+        )
+
+    def active_step(g, fresh, j):
         sums = []
         for which in range(2):
-            mine = product(which, 3, j).astype(jnp.bfloat16).astype(jnp.float32)
-            near_copy(which, j).wait_recv()
-            mine = mine + near_in[which, j].astype(jnp.float32)
-            far_copy(which, j).wait_recv()
-            sums.append(mine + far_in[which, j].astype(jnp.float32))
-        active[j] = (jax.nn.silu(sums[0]) * sums[1]).astype(jnp.bfloat16)
-        across_copy(j).start()
-        beside_copy(j).start()
-        lowered(active, 0, j)
-        beside_copy(j).wait_recv()
-        lowered(active_beside, 1, j)
-        return carry
-
-    lax.fori_loop(0, chunks, own_step, 0)
-
-    def last_step(j, carry):
-        across_copy(j).wait_recv()
-        diagonal_copy(j).start()
-        lowered(active_across, 2, j)
-        diagonal_copy(j).wait_recv()
-        lowered(active_diagonal, 3, j)
-        return carry
-
-    lax.fori_loop(0, chunks, last_step, 0)
-
-    for copy in outward:
-        copy.wait_send()
-    packed[...] = total[: peers * main].astype(jnp.bfloat16)
-    tail = total[peers * main :].astype(jnp.bfloat16)
-    folded = jnp.zeros((peers * SUB, piece), jnp.float32)
-    for part in range(fold):
-        folded = folded + jnp.dot(
-            refold(peers, extra, fold, part),
-            tail[:, part * piece : (part + 1) * piece],
-            preferred_element_type=jnp.float32,
-        )
-    packed_extra[...] = folded.astype(jnp.bfloat16)
-    homeward = travel((packed, packed_extra), (answers, answers_extra), -1, 2)
-    for copy in homeward:
-        copy.start()
+            mine = product(g, which, 3, j, fresh).astype(jnp.bfloat16).astype(jnp.float32)
+            near_copy(g, which, j).wait_recv()
+            mine = mine + near_in[g, which, j].astype(jnp.float32)
+            far_copy(g, which, j).wait_recv()
+            sums.append(mine + far_in[g, which, j].astype(jnp.float32))
+        active[g, j] = (jax.nn.silu(sums[0]) * sums[1]).astype(jnp.bfloat16)
+        across_copy(g, j).start()
+        beside_copy(g, j).start()
+
+    def lower_step(g, fresh, j):
+        lowered(g, active, 0, j, fresh)
+        beside_copy(g, j).wait_recv()
+        lowered(g, active_beside, 1, j, fresh)
+
+    def last_step(g, fresh, j):
+        across_copy(g, j).wait_recv()
+        diagonal_copy(g, j).start()
+        lowered(g, active_across, 2, j, fresh)
+        diagonal_copy(g, j).wait_recv()
+        lowered(g, active_diagonal, 3, j, fresh)
+
+    def send_home(g):
+        pack(g, total[g * group : (g + 1) * group, :])
+        for copy in travel(g, answers, answers_extra, 2):
+            copy.start()
+
+    receive_rows(0)
+    loop(functools.partial(far_step, 0, True))
+    receive_rows(1)
+    loop(functools.partial(far_step, 1, False))
+    total[...] = jnp.zeros_like(total)
+    loop(functools.partial(near_step, 0, True))
+    loop(functools.partial(near_step, 1, False))
+
+    def far_group(j):
+        active_step(1, True, j)
+        lower_step(1, True, j)
+
+    loop(far_group)
+    loop(functools.partial(active_step, 0, False))
+    for g in range(2):
+        for copy in travel(g, rows, rows_extra, 0):
+            copy.wait_send()
+    loop(functools.partial(last_step, 1, True))
+    send_home(1)
+    loop(functools.partial(lower_step, 0, False))
+    loop(functools.partial(last_step, 0, False))
+    send_home(0)
     answers[:main] = packed[:main]
     answers_extra[:SUB] = packed_extra[:SUB]
 
-    def drain(j, carry):
-        for which in range(2):
-            far_copy(which, j).wait_send()
-            near_copy(which, j).wait_send()
-        beside_copy(j).wait_send()
-        across_copy(j).wait_send()
-        diagonal_copy(j).wait_send()
-        return carry
-
-    lax.fori_loop(0, chunks, drain, 0)
-    for copy in homeward:
-        copy.wait_recv()
-    landed = answers_extra[...]
-    for part in range(fold):
-        answers[peers * main :, part * piece : (part + 1) * piece] = jnp.dot(
-            unfold(peers, extra, fold, part), landed, preferred_element_type=jnp.float32
-        ).astype(jnp.bfloat16)
+    def drain(j):
+        for g in range(2):
+            for which in range(2):
+                far_copy(g, which, j).wait_send()
+                near_copy(g, which, j).wait_send()
+            beside_copy(g, j).wait_send()
+            across_copy(g, j).wait_send()
+            diagonal_copy(g, j).wait_send()
+
+    loop(drain)
+    for g in (1, 0):
+        for copy in travel(g, answers, answers_extra, 2):
+            copy.wait_recv()
+        unpack(g, answers, answers_extra)
     routed = jnp.dot(weights_high[...], answers[...], preferred_element_type=jnp.float32)
     routed = routed + jnp.dot(weights_low[...], answers[...], preferred_element_type=jnp.float32)
     out[...] = (hidden[...].astype(jnp.float32) + routed).astype(jnp.bfloat16)
-    for copy in homeward:
-        copy.wait_send()
+    for g in range(2):
+        for copy in travel(g, answers, answers_extra, 2):
+            copy.wait_send()
 
 
 def block_direct(
@@ -843,7 +891,7 @@
     count = peers * CAP
     vmem = pl.BlockSpec(memory_space=pltpu.VMEM)
     anywhere = pl.BlockSpec(memory_space=pl.ANY)
-    block = (chunks, count, CHUNK)
+    block = (chunks, count // 2, CHUNK)
     low = jnp.bfloat16
     return pl.pallas_call(
         functools.partial(block_kernel, peers),
@@ -880,15 +928,15 @@
             pltpu.VMEM((peers * SUB, width * extra // SUB), low),
             pltpu.VMEM((count, width), low),
             pltpu.VMEM((peers * SUB, width * extra // SUB), low),
+            pltpu.VMEM((2, 2) + block, low),
+            pltpu.VMEM((2, 2) + block, low),
+            pltpu.VMEM((2, 2) + block, low),
+            pltpu.VMEM((2, 2) + block, low),
+            pltpu.VMEM((2, 2) + block, low),
             pltpu.VMEM((2,) + block, low),
             pltpu.VMEM((2,) + block, low),
             pltpu.VMEM((2,) + block, low),
             pltpu.VMEM((2,) + block, low),
-            pltpu.VMEM((2,) + block, low),
-            pltpu.VMEM(block, low),
-            pltpu.VMEM(block, low),
-            pltpu.VMEM(block, low),
-            pltpu.VMEM(block, low),
             pltpu.VMEM((count, width), jnp.float32),
             pltpu.SemaphoreType.DMA((12, chunks)),
             pltpu.SemaphoreType.DMA((2,)),
@@ -907,8 +955,8 @@
             pltpu.SemaphoreType.DMA((2, 3)),
             pltpu.SemaphoreType.DMA((4, peers)),
             pltpu.SemaphoreType.DMA((4, peers)),
-            pltpu.SemaphoreType.DMA((9, chunks)),
-            pltpu.SemaphoreType.DMA((9, chunks)),
+            pltpu.SemaphoreType.DMA((2, 9, chunks)),
+            pltpu.SemaphoreType.DMA((2, 9, chunks)),
         ],
         compiler_params=pltpu.CompilerParams(
             collective_id=0, has_side_effects=True, vmem_limit_bytes=66_000_000
@@ -917,8 +965,8 @@
     )(
         mixer_input,
         gate_input,
-        state_proj,
-        step_raw,
+        state_proj.T,
+        step_raw.T,
         conv_weight,
         conv_state_weight,
         step_bias[None, :],
@@ -927,8 +975,8 @@
         mixer_gain[None, :],
         residual,
         feed_gain[None, :],
-        expert_ids,
-        expert_weights,
+        expert_ids.T,
+        expert_weights.T,
         out_weight,
         gate,
         up,

time: 175 us -> 158 us (0.903)
  Pallas kernels: 168 us -> 157 us
  local copies, waits for them, and re-layouts: 7.3 us -> 1.67 us
    pallas_call x1, Pallas kernels: 168 us -> 157 us  [block_direct(): pl.pallas_call(functools.partial(block_kernel, peers), out_shape=jax.Shap...]
    unnamed x5 -> x1, local copies, waits for them, and re-layouts: 7.3 us -> 1.67 us
where the time goes in v3:
time: 158 us
  Pallas kernels  157 us (99%)
  local copies, waits for them, and re-layouts  1.67 us (1%)
    pallas_call x1, Pallas kernels, block_direct(): pl.pallas_call(functools.partial(block_kernel, peers), out_shape=jax.Shap...  157 us

profile of v3, /device:TPU:0, one launch (start us, length us, event | category | flops | bytes accessed | tf_op | source)
XLA Modules:
  0.0 158.2 jit_solution(17706411991935961989)
XLA Ops:
  0.0 156.6 %block.1 = bf16[128,1024]{1,0:T(8,128)(2,1)} custom-call(bf16[128,1024]{1,0:T(8,128)(2,1)} %mixer_input.1, bf16[128,1024]{1,0:T(8,128)(2,1)} %gate_input.1, bf16[32,128]{1,0:T(8,128)(2,1)} %bitcast.9, f32[16,128]{1,0:T(8,128)} %bitcast.10, f32[4,1024]{1,0:T(4,128)} %conv_weight.1, f32[4,32]{1,0:T(4,128)} %conv_state_weight.1, f32[1,16]{1,0:T(1,128)} %bitcast.15, ...), custom_call_target="tpu_custom_call" | custom-call | tf_op jit(solution)/shard_map/block/pallas_call | solution.py:896
  156.6 1.7 %copy.20 = bf16[128,1024]{1,0:T(8,128)(2,1)} copy(bf16[128,1024]{1,0:T(8,128)(2,1)} %block.1) | data formatting | bytes 524288

commit v4 on v3

--- a/solution.py
+++ b/solution.py
@@ -148,6 +148,7 @@
     tail_in,
     entering_state,
     logs,
+    kept,
     gate_tiles,
     up_tiles,
     down_tiles,
@@ -504,10 +505,6 @@
 
     for n in range(3):
         stats_copy(0, n).start()
-    for n in range(2):
-        weight_copy(n).wait()
-    for n in range(pieces):
-        weight_across(n).wait_recv()
 
     def give_copy(b):
         return remote(slab(0, b), slab(1, b), merge_send.at[0, b], merge_receive.at[0, b], {"tp": beside})
@@ -530,13 +527,15 @@
     def store(kind, b, data):
         held[line // 2 + kind, pl.ds(pl.multiple_of(b * half, half), half), :] = data
 
-    def forward(b, direction):
-        for h in range(2):
+    def forward(h):
+        def action(b, direction):
             line_copy(direction, b, h).wait_recv()
 
             @pl.when((z < line - 1) if direction == 0 else (z > 0))
             def _():
                 line_copy(direction, b, h).start()
+
+        return action
 
     def multiply(b, slot):
         block = held[b // 2, pl.ds(pl.multiple_of(b % 2 * tokens, tokens), tokens), :]
@@ -559,13 +558,13 @@
 
         @pl.when(side == z // 2)
         def _():
-            total[mine(slot), :] = joint
+            kept[b] = joint
 
     def deliver(b, slot):
         @pl.when(side == z // 2)
         def _():
             cross_copy(b).wait_recv()
-            joint = (total[mine(slot), :] + slab(3, b)[...].astype(jnp.float32)).astype(jnp.bfloat16)
+            joint = (kept[b] + slab(3, b)[...].astype(jnp.float32)).astype(jnp.bfloat16)
             stays = jnp.logical_and(b == z, tp == z)
 
             @pl.when(stays)
@@ -590,12 +589,26 @@
         def _():
             action(z + step, 1)
 
-    for step in range(line):
-        if step > 0:
-            each(step, forward)
-            each(step - 1, deliver)
+    def gather(step):
+        for h in range(2):
+            each(step, forward(h))
+
+    gather(1)
+    for n in range(2):
+        weight_copy(n).wait()
+    for n in range(pieces):
+        weight_across(n).wait_recv()
+    each(0, multiply)
+    each(0, merge)
+    for step in range(1, line):
+        if step == 1:
+            for ahead in range(2, line - 1):
+                gather(ahead)
+        elif step == line - 1:
+            gather(step)
         each(step, multiply)
         each(step, merge)
+        each(step - 1, deliver)
     each(line - 1, deliver)
 
     scale = stats_total(0)
@@ -803,12 +816,25 @@
         beside_copy(g, j).wait_recv()
         lowered(g, active_beside, 1, j, fresh)
 
-    def last_step(g, fresh, j):
+    def across_step(g, fresh, j):
         across_copy(g, j).wait_recv()
         diagonal_copy(g, j).start()
         lowered(g, active_across, 2, j, fresh)
+
+    def diagonal_step(g, fresh, j):
         diagonal_copy(g, j).wait_recv()
         lowered(g, active_diagonal, 3, j, fresh)
+
+    def last_steps(g, fresh):
+        across_step(g, fresh, 0)
+
+        def run(j, carry):
+            across_step(g, fresh, j)
+            diagonal_step(g, fresh, j - 1)
+            return carry
+
+        lax.fori_loop(1, chunks, run, 0)
+        diagonal_step(g, fresh, chunks - 1)
 
     def send_home(g):
         pack(g, total[g * group : (g + 1) * group, :])
@@ -832,10 +858,10 @@
     for g in range(2):
         for copy in travel(g, rows, rows_extra, 0):
             copy.wait_send()
-    loop(functools.partial(last_step, 1, True))
+    last_steps(1, True)
     send_home(1)
     loop(functools.partial(lower_step, 0, False))
-    loop(functools.partial(last_step, 0, False))
+    last_steps(0, False)
     send_home(0)
     answers[:main] = packed[:main]
     answers_extra[:SUB] = packed_extra[:SUB]
@@ -919,6 +945,7 @@
             pltpu.VMEM((peers, 8, tokens), jnp.float32),
             pltpu.VMEM((2 * states, width), jnp.float32),
             pltpu.VMEM((8, tokens), jnp.float32),
+            pltpu.VMEM((peers // 2, tokens // 2, width), jnp.float32),
             pltpu.VMEM((4, chunks, width, CHUNK), low),
             pltpu.VMEM((4, chunks, width, CHUNK), low),
             pltpu.VMEM((4, chunks, CHUNK, width), low),
@@ -959,7 +986,7 @@
             pltpu.SemaphoreType.DMA((2, 9, chunks)),
         ],
         compiler_params=pltpu.CompilerParams(
-            collective_id=0, has_side_effects=True, vmem_limit_bytes=66_000_000
+            collective_id=0, has_side_effects=True, vmem_limit_bytes=67_000_000
         ),
         name="block",
     )(

time: 158 us -> 151 us (0.956)
  Pallas kernels: 157 us -> 148 us
    pallas_call x1, Pallas kernels: 157 us -> 148 us  [block_direct(): pl.pallas_call(functools.partial(block_kernel, peers), out_shape=jax.Shap...]
where the time goes in v4:
time: 151 us; the launch traced here: 150 us
  Pallas kernels  148 us (98%)
  local copies, waits for them, and re-layouts  1.67 us (1%)
    pallas_call x1, Pallas kernels, block_direct(): pl.pallas_call(functools.partial(block_kernel, peers), out_shape=jax.Shap...  148 us

profile of v4, /device:TPU:0, one launch (start us, length us, event | category | flops | bytes accessed | tf_op | source)
XLA Modules:
  0.0 149.8 jit_solution(12945994353690261438)
XLA Ops:
  0.0 148.1 %block.1 = bf16[128,1024]{1,0:T(8,128)(2,1)} custom-call(bf16[128,1024]{1,0:T(8,128)(2,1)} %mixer_input.1, bf16[128,1024]{1,0:T(8,128)(2,1)} %gate_input.1, bf16[32,128]{1,0:T(8,128)(2,1)} %bitcast.9, f32[16,128]{1,0:T(8,128)} %bitcast.10, f32[4,1024]{1,0:T(4,128)} %conv_weight.1, f32[4,32]{1,0:T(4,128)} %conv_state_weight.1, f32[1,16]{1,0:T(1,128)} %bitcast.15, ...), custom_call_target="tpu_custom_call" | custom-call | tf_op jit(solution)/shard_map/block/pallas_call | solution.py:922
  148.1 1.7 %copy.20 = bf16[128,1024]{1,0:T(8,128)(2,1)} copy(bf16[128,1024]{1,0:T(8,128)(2,1)} %block.1) | data formatting | bytes 524288
